TPU v7x, 32 devices: a whole 2x2x4 slice. The times are simulated.
32 devices in a mesh: dp: 8 (over y, x, core), ctx: 4 (over z).
Axes of the slice: x: 2, y: 2, z: 4, core: 2. Of those that a mesh axis runs over, the one named last changes fastest.
Arguments:
- inputs: bfloat16 [2, 8192, 768], P(None, ('dp', 'ctx')), may hold values from -6 to 6
- cotangent: bfloat16 [2, 8192, 768], P(None, ('dp', 'ctx')), may hold values from -6 to 6
- lengths: int32 [2, 8, 4], P(None, 'dp'), may hold values from 1 to 896, 1024 in all within a row
- send_order: int32 [2, 32, 256], P(None, ('dp', 'ctx')), may hold values from 0 to 255, each once within a row
- norm1_gain: bfloat16 [768], P(('dp', 'ctx')), may hold values from 0.099609375 to 1.8984375
- qkv_weight: bfloat16 [768, 2304], P(('dp', 'ctx')), may hold values from -0.3125 to 0.3125
- out_weight: bfloat16 [768, 768], P(('dp', 'ctx')), may hold values from -1.25 to 1.25
- norm2_gain: bfloat16 [768], P(('dp', 'ctx')), may hold values from 0.099609375 to 1.8984375
- gate_weight: bfloat16 [768, 2048], P(('dp', 'ctx')), may hold values from -0.21875 to 0.21875
- up_weight: bfloat16 [768, 2048], P(('dp', 'ctx')), may hold values from -0.21875 to 0.21875
- down_weight: bfloat16 [2048, 768], P(('dp', 'ctx')), may hold values from -0.1875 to 0.1875
Outputs:
- layer_out: bfloat16 [2, 8192, 768], P(None, ('dp', 'ctx'))
- input_grad: bfloat16 [2, 8192, 768], P(None, ('dp', 'ctx'))
- norm1_grad: float32 [768], P(('dp', 'ctx'))
- qkv_grad: float32 [768, 2304], P(('dp', 'ctx'))
- out_grad: float32 [768, 768], P(('dp', 'ctx'))
- norm2_grad: float32 [768], P(('dp', 'ctx'))
- gate_grad: float32 [768, 2048], P(('dp', 'ctx'))
- up_grad: float32 [768, 2048], P(('dp', 'ctx'))
- down_grad: float32 [2048, 768], P(('dp', 'ctx'))
Inputs may be any that keep to these rules, and one draw needn't show every extreme that they name: Each pack's 4 lengths sum to 1024, and the longest of each pack has 896. `send_order`: each row of 256 entries holds every number of 0 to 255 once.
All inputs are finite; a program needn't handle non-finite values.
Results may differ from a plain program's by a relative error of at most 0.015.
The roundings to bfloat16 on the way count: a program that leaves them out, or rounds other values in their place, can miss the bound.
Values may be sent and summed in bfloat16 or wider, within the bound.
A program may use at most 192 MiB of HBM per device.

v0:
```python
import jax
import jax.numpy as jnp
from jax import lax
from jax.sharding import PartitionSpec as P

HEADS = 12


eps_norm = 1e-05
rope_base = 10000.0


def scaled_norm(values, gain):
    inverse = lax.rsqrt(jnp.mean(values * values, axis=-1, keepdims=True) + eps_norm)
    return values * inverse * gain


def swish_product(gate_value, up_value):
    return jax.nn.silu(gate_value) * up_value


def pack_layout(seq_lengths, row_ids):
    seq_ends = jnp.cumsum(seq_lengths)
    passed = (row_ids[:, None] >= seq_ends[None, :]).astype(jnp.int32)
    segment = jnp.sum(passed, axis=1)
    seq_start = jnp.sum(passed * seq_lengths[None, :], axis=1)
    return (segment, row_ids - seq_start)


def rope_tables(position, head_size):
    half_dim = head_size // 2
    frequency = rope_base ** (-(jnp.arange(half_dim, dtype=jnp.float32) * 2.0 / head_size))
    angles = position.astype(jnp.float32)[:, None] * frequency[None, :]
    return (jnp.cos(angles), jnp.sin(angles))


def rotate(values, cosine, sine, head_count):
    shaped = values.reshape(values.shape[0], head_count, -1)
    half_dim = shaped.shape[-1] // 2
    first_half = shaped[..., :half_dim]
    second_half = shaped[..., half_dim:]
    cos_wide = cosine[:, None, :]
    sin_wide = sine[:, None, :]
    turned = jnp.concatenate(
        [
            first_half * cos_wide - second_half * sin_wide,
            second_half * cos_wide + first_half * sin_wide,
        ],
        axis=-1,
    )
    return turned.reshape(values.shape)


def split_heads(array, head_count):
    return array.reshape(array.shape[0], head_count, -1).transpose(1, 0, 2)


def join_heads(array):
    return array.transpose(1, 0, 2).reshape(array.shape[1], -1)


def head_forward(member, allowed, score_scale):
    queries, keys, values = member
    scores = (
        jnp.einsum("qd,kd->qk", queries, keys, preferred_element_type=jnp.float32) * score_scale
    )
    scores = jnp.where(allowed, scores, -jnp.inf)
    row_max = jnp.max(scores, axis=1, keepdims=True)
    shifted = jnp.exp(scores - row_max)
    row_sum = jnp.sum(shifted, axis=1, keepdims=True)
    soft_probs = (shifted / row_sum).astype(jnp.bfloat16)
    mixture = jnp.dot(soft_probs, values, preferred_element_type=jnp.float32)
    return (mixture, row_max, row_sum)


def head_backward(member, allowed, score_scale):
    queries, keys, values, grad_mix, row_max, row_sum = member
    scores = (
        jnp.einsum("qd,kd->qk", queries, keys, preferred_element_type=jnp.float32) * score_scale
    )
    scores = jnp.where(allowed, scores, -jnp.inf)
    soft = jnp.exp(scores - row_max) / row_sum
    grad_soft = jnp.einsum("qd,kd->qk", grad_mix, values, preferred_element_type=jnp.float32)
    grad_values = jnp.einsum(
        "qk,qd->kd", soft.astype(jnp.bfloat16), grad_mix, preferred_element_type=jnp.float32
    )
    weighted = jnp.sum(soft * grad_soft, axis=1, keepdims=True)
    grad_scores = (soft * (grad_soft - weighted)).astype(jnp.bfloat16)
    grad_queries = jnp.dot(grad_scores, keys, preferred_element_type=jnp.float32) * score_scale
    grad_keys = (
        jnp.einsum("qk,qd->kd", grad_scores, queries, preferred_element_type=jnp.float32)
        * score_scale
    )
    return (grad_queries, grad_keys, grad_values)


def per_device(
    inputs,
    cotangent,
    lengths,
    send_order,
    norm1_gain,
    qkv_weight,
    out_weight,
    norm2_gain,
    gate_weight,
    up_weight,
    down_weight,
):
    micro_count = inputs.shape[0]
    tok_rows = inputs.shape[1]
    model_width = inputs.shape[2]
    peer_count = lax.axis_size("dp")
    slot_rows = tok_rows // peer_count
    group_rows = tok_rows * lax.axis_size("ctx")
    head_size = model_width // HEADS
    score_scale = head_size ** (-0.5)
    shards = (norm1_gain, qkv_weight, out_weight, norm2_gain, gate_weight, up_weight, down_weight)
    query_rows = lax.axis_index("ctx") * tok_rows + jnp.arange(tok_rows, dtype=jnp.int32)
    key_rows = jnp.arange(group_rows, dtype=jnp.int32)
    shares = tuple((jnp.zeros(piece.shape, jnp.float32) for piece in shards))
    outs_list = []
    grads_list = []
    for step_index in range(micro_count):
        row_order = send_order[step_index, 0]
        sent_x = jnp.take(inputs[step_index], row_order, axis=0).reshape(
            peer_count, slot_rows, model_width
        )
        sent_dy = jnp.take(cotangent[step_index], row_order, axis=0).reshape(
            peer_count, slot_rows, model_width
        )
        got_x, got_dy = (
            lax.all_to_all(sent_x, "dp", split_axis=0, concat_axis=0, tiled=True),
            lax.all_to_all(sent_dy, "dp", split_axis=0, concat_axis=0, tiled=True),
        )
        local_x = got_x.reshape(tok_rows, model_width).astype(jnp.float32)
        grad_out = got_dy.reshape(tok_rows, model_width).astype(jnp.float32)
        seq_lengths = lengths[step_index, 0]
        seg_query, pos_query = pack_layout(seq_lengths, query_rows)
        seg_key, unused_pos = pack_layout(seq_lengths, key_rows)
        allowed = (seg_query[:, None] == seg_key[None, :]) & (
            key_rows[None, :] <= query_rows[:, None]
        )
        cosine, sine = rope_tables(pos_query, head_size)
        weights_now = (
            lax.all_gather(shards[0], ("dp", "ctx"), axis=0, tiled=True),
            lax.all_gather(shards[1], ("dp", "ctx"), axis=0, tiled=True),
            lax.all_gather(shards[2], ("dp", "ctx"), axis=0, tiled=True),
            lax.all_gather(shards[3], ("dp", "ctx"), axis=0, tiled=True),
            lax.all_gather(shards[4], ("dp", "ctx"), axis=0, tiled=True),
            lax.all_gather(shards[5], ("dp", "ctx"), axis=0, tiled=True),
            lax.all_gather(shards[6], ("dp", "ctx"), axis=0, tiled=True),
        )
        gain_first, wqkv, wout, gain_second, wgate, wup, wdown = weights_now
        normed1 = scaled_norm(local_x, gain_first.astype(jnp.float32)).astype(jnp.bfloat16)
        qkv = jnp.dot(normed1, wqkv, preferred_element_type=jnp.float32)
        queries = rotate(qkv[:, :model_width], cosine, sine, HEADS).astype(jnp.bfloat16)
        keys = rotate(qkv[:, model_width : 2 * model_width], cosine, sine, HEADS).astype(
            jnp.bfloat16
        )
        values = qkv[:, 2 * model_width :].astype(jnp.bfloat16)
        key_value = jnp.concatenate([keys, values], axis=1)
        gathered = lax.all_gather(key_value, "ctx", axis=0, tiled=True)
        query_heads = split_heads(queries, HEADS)
        key_heads = split_heads(gathered[:, :model_width], HEADS)
        value_heads = split_heads(gathered[:, model_width:], HEADS)
        mixture, row_maxes, row_sums = lax.map(
            lambda member: head_forward(member, allowed, score_scale),
            (query_heads, key_heads, value_heads),
        )
        attended = join_heads(mixture).astype(jnp.bfloat16)
        hidden = local_x + jnp.dot(attended, wout, preferred_element_type=jnp.float32)
        gain_two = gain_second.astype(jnp.float32)
        normed2 = scaled_norm(hidden, gain_two).astype(jnp.bfloat16)
        gate_value = jnp.dot(normed2, wgate, preferred_element_type=jnp.float32)
        up_value = jnp.dot(normed2, wup, preferred_element_type=jnp.float32)
        inner_act = swish_product(gate_value, up_value).astype(jnp.bfloat16)
        result = hidden + jnp.dot(inner_act, wdown, preferred_element_type=jnp.float32)
        layer_out = result.astype(jnp.bfloat16)
        weights_back = (
            lax.all_gather(shards[0], ("dp", "ctx"), axis=0, tiled=True),
            lax.all_gather(shards[1], ("dp", "ctx"), axis=0, tiled=True),
            lax.all_gather(shards[2], ("dp", "ctx"), axis=0, tiled=True),
            lax.all_gather(shards[3], ("dp", "ctx"), axis=0, tiled=True),
            lax.all_gather(shards[4], ("dp", "ctx"), axis=0, tiled=True),
            lax.all_gather(shards[5], ("dp", "ctx"), axis=0, tiled=True),
            lax.all_gather(shards[6], ("dp", "ctx"), axis=0, tiled=True),
        )
        gain_first_b, wqkv_b, wout_b, gain_second_b, wgate_b, wup_b, wdown_b = weights_back
        g_down = grad_out.astype(jnp.bfloat16)
        d_down = jnp.einsum("tf,td->fd", inner_act, g_down, preferred_element_type=jnp.float32)
        grad_inner = jnp.einsum("td,fd->tf", g_down, wdown_b, preferred_element_type=jnp.float32)
        unused_act, swish_back = jax.vjp(swish_product, gate_value, up_value)
        grad_gate, grad_up = swish_back(grad_inner)
        g_gate = grad_gate.astype(jnp.bfloat16)
        g_up = grad_up.astype(jnp.bfloat16)
        d_gate = jnp.einsum("td,tf->df", normed2, g_gate, preferred_element_type=jnp.float32)
        d_up = jnp.einsum("td,tf->df", normed2, g_up, preferred_element_type=jnp.float32)
        grad_normed2 = jnp.einsum(
            "tf,df->td", g_gate, wgate_b, preferred_element_type=jnp.float32
        ) + jnp.einsum("tf,df->td", g_up, wup_b, preferred_element_type=jnp.float32)
        unused_norm, norm2_back = jax.vjp(scaled_norm, hidden, gain_second_b.astype(jnp.float32))
        grad_hidden_n, d_gain2 = norm2_back(grad_normed2)
        grad_hidden = grad_out + grad_hidden_n
        g_branch = grad_hidden.astype(jnp.bfloat16)
        d_out = jnp.einsum("td,te->de", attended, g_branch, preferred_element_type=jnp.float32)
        grad_attended = jnp.einsum(
            "te,de->td", g_branch, wout_b, preferred_element_type=jnp.float32
        ).astype(jnp.bfloat16)
        gathered_back = lax.all_gather(key_value, "ctx", axis=0, tiled=True)
        key_heads = split_heads(gathered_back[:, :model_width], HEADS)
        value_heads = split_heads(gathered_back[:, model_width:], HEADS)
        grad_heads = split_heads(grad_attended, HEADS)
        grad_q_heads, grad_k_heads, grad_v_heads = lax.map(
            lambda member: head_backward(member, allowed, score_scale),
            (query_heads, key_heads, value_heads, grad_heads, row_maxes, row_sums),
        )
        own_keys, own_values = (
            lax.psum_scatter(
                join_heads(grad_k_heads).astype(jnp.bfloat16),
                "ctx",
                scatter_dimension=0,
                tiled=True,
            ).astype(jnp.float32),
            lax.psum_scatter(
                join_heads(grad_v_heads).astype(jnp.bfloat16),
                "ctx",
                scatter_dimension=0,
                tiled=True,
            ).astype(jnp.float32),
        )
        grad_qkv = jnp.concatenate(
            [
                rotate(join_heads(grad_q_heads), cosine, -sine, HEADS),
                rotate(own_keys, cosine, -sine, HEADS),
                own_values,
            ],
            axis=1,
        ).astype(jnp.bfloat16)
        d_qkv = jnp.einsum("td,te->de", normed1, grad_qkv, preferred_element_type=jnp.float32)
        grad_normed1 = jnp.einsum("te,de->td", grad_qkv, wqkv_b, preferred_element_type=jnp.float32)
        unused_first, norm1_back = jax.vjp(scaled_norm, local_x, gain_first_b.astype(jnp.float32))
        grad_x_n, d_gain1 = norm1_back(grad_normed1)
        grad_input = (grad_hidden + grad_x_n).astype(jnp.bfloat16)
        back_out, back_grad = (
            lax.all_to_all(
                layer_out.reshape(peer_count, slot_rows, model_width),
                "dp",
                split_axis=0,
                concat_axis=0,
                tiled=True,
            ),
            lax.all_to_all(
                grad_input.reshape(peer_count, slot_rows, model_width),
                "dp",
                split_axis=0,
                concat_axis=0,
                tiled=True,
            ),
        )
        outs_list.append(
            jnp.zeros((tok_rows, model_width), jnp.bfloat16)
            .at[row_order]
            .set(back_out.reshape(tok_rows, model_width))
        )
        grads_list.append(
            jnp.zeros((tok_rows, model_width), jnp.bfloat16)
            .at[row_order]
            .set(back_grad.reshape(tok_rows, model_width))
        )
        grad_terms = (d_gain1, d_qkv, d_out, d_gain2, d_gate, d_up, d_down)
        owned = (
            lax.psum_scatter(grad_terms[0], ("dp", "ctx"), scatter_dimension=0, tiled=True),
            lax.psum_scatter(grad_terms[1], ("dp", "ctx"), scatter_dimension=0, tiled=True),
            lax.psum_scatter(grad_terms[2], ("dp", "ctx"), scatter_dimension=0, tiled=True),
            lax.psum_scatter(grad_terms[3], ("dp", "ctx"), scatter_dimension=0, tiled=True),
            lax.psum_scatter(grad_terms[4], ("dp", "ctx"), scatter_dimension=0, tiled=True),
            lax.psum_scatter(grad_terms[5], ("dp", "ctx"), scatter_dimension=0, tiled=True),
            lax.psum_scatter(grad_terms[6], ("dp", "ctx"), scatter_dimension=0, tiled=True),
        )
        shares = tuple((earlier + later for earlier, later in zip(shares, owned)))
    return (
        jnp.stack(outs_list),
        jnp.stack(grads_list),
        shares[0],
        shares[1],
        shares[2],
        shares[3],
        shares[4],
        shares[5],
        shares[6],
    )


def solution(mesh):
    in_specs = (
        P(None, ("dp", "ctx"), None),
        P(None, ("dp", "ctx"), None),
        P(None, "dp", None),
        P(None, ("dp", "ctx"), None),
        P(("dp", "ctx")),
        P(("dp", "ctx"), None),
        P(("dp", "ctx"), None),
        P(("dp", "ctx")),
        P(("dp", "ctx"), None),
        P(("dp", "ctx"), None),
        P(("dp", "ctx"), None),
    )
    out_specs = (
        P(None, ("dp", "ctx"), None),
        P(None, ("dp", "ctx"), None),
        P(("dp", "ctx")),
        P(("dp", "ctx"), None),
        P(("dp", "ctx"), None),
        P(("dp", "ctx")),
        P(("dp", "ctx"), None),
        P(("dp", "ctx"), None),
        P(("dp", "ctx"), None),
    )
    return jax.shard_map(
        per_device, mesh=mesh, in_specs=in_specs, out_specs=out_specs, check_vma=False
    )
```

profile of v0, /device:TPU:4, one launch (start us, length us, event | category | flops | bytes accessed | tf_op | source)
XLA Modules:
  0.0 1508.7 jit_solution(8477965118600745933)
XLA Ops:
  20.4 41.7 %all-reduce.5 = (bf16[768]{0:T(1024)(128)(2,1)S(1)}, bf16[768]{0:T(1024)(128)(2,1)S(1)}) all-reduce(bf16[768]{0:T(1024)(128)(2,1)S(1)} %dynamic-update-slice, bf16[768]{0:T(1024)(128)(2,1)S(1)} %dynamic-update-slice.1), channel_id=1, replica_groups=mesh['dp'=8,'ctx'=4] {'dp','ctx'}, use_global_device_ids=true, to_apply=%add | all-reduce | flops 1536 | bytes 6144
  64.1 9.8 all-gather.8.cloned.1.call-done
  88.1 54.5 %all-gather.10.cloned.1.call-done = bf16[1024,1536]{1,0:T(8,128)(2,1)} async-done(((bf16[256,1536]{1,0:T(8,128)(2,1)}), bf16[1024,1536]{1,0:T(8,128)(2,1)}) %all-gather.10.cloned.1.call-update) | async-done | bytes 3145744 | tf_op jit(solution)/shard_map/all_gather | solution.py:163
  158.3 38.1 %while.60 = (s32[]{:T(128)}, bf16[12,256,64]{1,2,0:T(8,128)(2,1)S(1)}, f32[12,256,1]{1,2,0:T(1,128)S(1)}, f32[12,256,1]{1,2,0:T(1,128)S(1)}, bf16[12,256,64]{2,1...) while((s32[]{:T(128)}, ...), condition=%wide.region_8.10_spmd.clone, body=%wide.region_5.9_spmd.clone.sunk | while | flops 69991936 | bytes 3818617 | solution.py:167
  201.0 57.9 %all-gather.14.cloned.1.call-done = bf16[768,2048]{1,0:T(8,128)(2,1)} async-done(((bf16[24,2048]{1,0:T(8,128)(2,1)}), bf16[768,2048]{1,0:T(8,128)(2,1)}) %all-gather.14.cloned.1.call-update) | async-done | bytes 3145744 | tf_op jit(solution)/shard_map/all_gather | solution.py:150
  263.1 56.4 %all-gather.16.cloned.1.call-done = bf16[768,2048]{1,0:T(8,128)(2,1)} async-done(((bf16[24,2048]{1,0:T(8,128)(2,1)}), bf16[768,2048]{1,0:T(8,128)(2,1)}) %all-gather.16.cloned.1.call-update) | async-done | bytes 3145744 | tf_op jit(solution)/shard_map/all_gather | solution.py:151
  323.7 56.5 %all-gather.18.cloned.1.call-done = bf16[2048,768]{1,0:T(8,128)(2,1)} async-done(((bf16[64,768]{1,0:T(8,128)(2,1)}), bf16[2048,768]{1,0:T(8,128)(2,1)}) %all-gather.18.cloned.1.call-update) | async-done | bytes 3145744 | tf_op jit(solution)/shard_map/all_gather | solution.py:152
  380.2 5.8 multiply_convert_fusion.3
  398.4 108.3 %while.62 = (s32[]{:T(128)}, f32[12,256,64]{1,2,0:T(8,128)}, bf16[12,1024,64]{1,2,0:T(8,128)(2,1)}, bf16[12,1024,64]{1,2,0:T(8,128)(2,1)}, bf16[12,256,64]{2,1,0...) while((s32[]{:T(128)}, f32[12,256,64]{1,2,0:T(8,128)}, ...), condition=%wide.region_25.27_spmd.clone, body=%wide.region_23.26_spmd.clone.sunk | while | flops 171261696 | bytes 9456785 | solution.py:214
  515.4 10.0 all_to_all.40
  526.4 14.5 reduce-scatter.10.cloned.1.call-done
  545.0 32.5 %reduce-scatter.12.cloned.1.call-done = bf16[256,768]{0,1:T(8,128)(2,1)} async-done(((bf16[1024,768]{0,1:T(8,128)(2,1)}), bf16[256,768]{0,1:T(8,128)(2,1)}) %reduce-scatter.12.cloned.1.call-update) | async-done | bytes 393232 | tf_op jit(solution)/shard_map/reduce_scatter | solution.py:225
  604.0 54.7 %all-gather.20.cloned.1.call-done = bf16[1024,1536]{1,0:T(8,128)(2,1)} async-done(((bf16[256,1536]{1,0:T(8,128)(2,1)}), bf16[1024,1536]{1,0:T(8,128)(2,1)}) %all-gather.20.cloned.1.call-update) | async-done | bytes 3145744 | tf_op jit(solution)/shard_map/all_gather | solution.py:163
  677.1 47.1 %while.61 = (s32[]{:T(128)}, bf16[12,256,64]{1,2,0:T(8,128)(2,1)}, f32[12,256,1]{1,2,0:T(1,128)}, f32[12,256,1]{1,2,0:T(1,128)}, bf16[12,256,64]{2,1,0:T(8,128)(...) while((s32[]{:T(128)}, bf16[12,256,64]{1,2,0:T(8,128)(2,1)}, ...), condition=%wide.region_19.21_spmd.clone, body=%wide.region_16.20_spmd.clone.sunk | while | flops 69991936 | bytes 6964401 | solution.py:167
  732.1 5.9 multiply_convert_fusion.2
  745.6 91.8 %while.63 = (s32[]{:T(128)}, f32[12,256,64]{1,2,0:T(8,128)}, bf16[12,1024,64]{1,2,0:T(8,128)(2,1)S(1)}, bf16[12,1024,64]{1,2,0:T(8,128)(2,1)}, bf16[12,256,64]{2...) while((s32[]{:T(128)}, f32[12,256,64]{1,2,0:T(8,128)}, ...), condition=%wide.region_33.35_spmd.clone, body=%wide.region_31.34_spmd.clone.sunk | while | flops 171261696 | bytes 9456785 | solution.py:214
  866.5 6.2 reduce-scatter.14.cloned.1.call-done
  875.3 34.0 %reduce-scatter.16.cloned.1.call-done = bf16[256,768]{0,1:T(8,128)(2,1)} async-done(((bf16[1024,768]{0,1:T(8,128)(2,1)}), bf16[256,768]{0,1:T(8,128)(2,1)}) %reduce-scatter.16.cloned.1.call-update) | async-done | bytes 393232 | tf_op jit(solution)/shard_map/reduce_scatter | solution.py:225
  909.3 7.1 convolution_add_fusion
  969.1 40.6 %all-reduce.4 = (f32[768]{0:T(1024)S(1)}, f32[768]{0:T(1024)S(1)}) all-reduce(f32[768]{0:T(1024)S(1)} %add.270, f32[768]{0:T(1024)S(1)} %add.273), channel_id=13, replica_groups=mesh['dp'=8,'ctx'=4] {'dp','ctx'}, use_global_device_ids=true, to_apply=%region_39.41.clone | all-reduce | flops 1536 | bytes 12288
  1016.0 120.9 %reduce-scatter.22.cloned.1.call-done = f32[24,2048]{1,0:T(8,128)} async-done(((f32[768,2048]{1,0:T(8,128)}), f32[24,2048]{1,0:T(8,128)}) %reduce-scatter.22.cloned.1.call-update) | async-done | bytes 196624 | tf_op jit(solution)/shard_map/reduce_scatter | solution.py:277
  1136.9 119.8 %reduce-scatter.24.cloned.1.call-done = f32[24,2048]{1,0:T(8,128)} async-done(((f32[768,2048]{1,0:T(8,128)}), f32[24,2048]{1,0:T(8,128)}) %reduce-scatter.24.cloned.1.call-update) | async-done | bytes 196624 | tf_op jit(solution)/shard_map/reduce_scatter | solution.py:278
  1256.7 120.8 %reduce-scatter.26.cloned.1.call-done = f32[64,768]{1,0:T(8,128)} async-done(((f32[2048,768]{1,0:T(8,128)}), f32[64,768]{1,0:T(8,128)}) %reduce-scatter.26.cloned.1.call-update) | async-done | bytes 196624 | tf_op jit(solution)/shard_map/reduce_scatter | solution.py:279
  1377.5 124.4 %reduce-scatter.18.cloned.1.call-done = f32[24,2304]{1,0:T(8,128)} async-done(((f32[768,2304]{1,0:T(8,128)}), f32[24,2304]{1,0:T(8,128)}) %reduce-scatter.18.cloned.1.call-update) | async-done | bytes 221200 | tf_op jit(solution)/shard_map/reduce_scatter | solution.py:274
  (679 shorter events, 518.3 us)
Async XLA Ops:
  7.2 66.7 %all-gather.8.cloned.1.call-start = ((), (), s32[]{:S(2)}) async-start(), calls=%async_computation.17 | async-start | bytes 3649536 | tf_op jit(solution)/shard_map/all_gather | solution.py:147
  14.6 48.4 %all-to-all-start = ((bf16[8,32,768]{2,1,0:T(8,128)(2,1)}), bf16[8,32,768]{2,1,0:T(8,128)(2,1)S(1)}, u32[]{:S(2)}, u32[]{:S(2)}) async-start(bf16[8,32,768]{2,1,0:T(8,128)(2,1)} %bitcast.4), calls=%async_computation | async-start | bytes 786432 | tf_op jit(solution)/shard_map/all_to_all | solution.py:133
  18.9 123.6 %all-gather.10.cloned.1.call-start = ((), (), s32[]{:S(2)}) async-start(), calls=%async_computation.18 | async-start | bytes 3932160 | tf_op jit(solution)/shard_map/all_gather | solution.py:163
  63.1 135.1 %copy-start.21 = (bf16[8,32,768]{2,1,0:T(8,128)(2,1)}, bf16[8,32,768]{2,1,0:T(8,128)(2,1)S(1)}, u32[]{:S(2)}) copy-start(bf16[8,32,768]{2,1,0:T(8,128)(2,1)S(1)} %all-to-all-done) | copy-start | bytes 1179652
  79.9 118.2 %all-gather.12.cloned.1.call-start = ((), (), s32[]{:S(2)}) async-start(), calls=%async_computation.19 | async-start | bytes 1216512 | tf_op jit(solution)/shard_map/all_gather | solution.py:148
  80.6 178.3 %all-gather.14.cloned.1.call-start = ((), (), s32[]{:S(2)}) async-start(), calls=%async_computation.20 | async-start | bytes 3244032 | tf_op jit(solution)/shard_map/all_gather | solution.py:150
  81.2 238.3 %all-gather.16.cloned.1.call-start = ((), (), s32[]{:S(2)}) async-start(), calls=%async_computation.21 | async-start | bytes 3244032 | tf_op jit(solution)/shard_map/all_gather | solution.py:151
  81.8 241.9 %all-to-all-start.4 = ((bf16[8,32,768]{2,1,0:T(8,128)(2,1)}), bf16[8,32,768]{2,1,0:T(8,128)(2,1)S(1)}, u32[]{:S(2)}, u32[]{:S(2)}) async-start(bf16[8,32,768]{2,1,0:T(8,128)(2,1)} %bitcast.45), calls=%async_computation.4 | async-start | bytes 786432 | tf_op jit(solution)/shard_map/all_to_all | solution.py:134
  85.9 294.2 %all-gather.18.cloned.1.call-start = ((), (), s32[]{:S(2)}) async-start(), calls=%async_computation.22 | async-start | bytes 3244032 | tf_op jit(solution)/shard_map/all_gather | solution.py:152
  86.5 454.4 %reduce-scatter.10.cloned.1.call-start = ((), (), s32[]{:S(2)}) async-start(), calls=%async_computation.24 | async-start | bytes 1966080 | tf_op jit(solution)/shard_map/reduce_scatter | solution.py:219
  506.7 70.9 %reduce-scatter.12.cloned.1.call-start = ((), (), s32[]{:S(2)}) async-start(), calls=%async_computation.25 | async-start | bytes 1966080 | tf_op jit(solution)/shard_map/reduce_scatter | solution.py:225
  507.4 151.3 %all-gather.20.cloned.1.call-start = ((), (), s32[]{:S(2)}) async-start(), calls=%async_computation.23 | async-start | bytes 3932160 | tf_op jit(solution)/shard_map/all_gather | solution.py:163
  596.1 135.9 %all-to-all-start.6 = ((bf16[8,32,768]{2,1,0:T(8,128)(2,1)}), bf16[8,32,768]{2,1,0:T(8,128)(2,1)}, u32[]{:S(2)}, u32[]{:S(2)}) async-start(bf16[8,32,768]{2,1,0:T(8,128)(2,1)} %bitcast.64), calls=%async_computation.8 | async-start | bytes 786432 | tf_op jit(solution)/shard_map/all_to_all | solution.py:134
  600.7 272.0 %reduce-scatter.14.cloned.1.call-start = ((), (), s32[]{:S(2)}) async-start(), calls=%async_computation.26 | async-start | bytes 1966080 | tf_op jit(solution)/shard_map/reduce_scatter | solution.py:219
  838.6 70.7 %reduce-scatter.16.cloned.1.call-start = ((), (), s32[]{:S(2)}) async-start(), calls=%async_computation.27 | async-start | bytes 1966080 | tf_op jit(solution)/shard_map/reduce_scatter | solution.py:225
  839.3 176.7 %reduce-scatter.20.cloned.1.call-start = ((), (), s32[]{:S(2)}) async-start(), calls=%async_computation.29 | async-start | bytes 2433024 | tf_op jit(solution)/shard_map/reduce_scatter | solution.py:275
  841.8 295.1 %reduce-scatter.22.cloned.1.call-start = ((), (), s32[]{:S(2)}) async-start(), calls=%async_computation.30 | async-start | bytes 6488064 | tf_op jit(solution)/shard_map/reduce_scatter | solution.py:277
  848.0 408.8 %reduce-scatter.24.cloned.1.call-start = ((), (), s32[]{:S(2)}) async-start(), calls=%async_computation.31 | async-start | bytes 6488064 | tf_op jit(solution)/shard_map/reduce_scatter | solution.py:278
  853.8 523.7 %reduce-scatter.26.cloned.1.call-start = ((), (), s32[]{:S(2)}) async-start(), calls=%async_computation.32 | async-start | bytes 6488064 | tf_op jit(solution)/shard_map/reduce_scatter | solution.py:279
  861.2 640.7 %reduce-scatter.18.cloned.1.call-start = ((), (), s32[]{:S(2)}) async-start(), calls=%async_computation.28 | async-start | bytes 7299072 | tf_op jit(solution)/shard_map/reduce_scatter | solution.py:274
  921.2 11.5 all-to-all-start.1
  932.7 12.5 all-to-all-start.5
  945.2 11.9 all-to-all-start.3
  957.1 53.8 %all-to-all-start.7 = ((bf16[8,32,768]{2,1,0:T(8,128)(2,1)}), bf16[8,32,768]{2,1,0:T(8,128)(2,1)S(1)}, u32[]{:S(2)}, u32[]{:S(2)}) async-start(bf16[8,32,768]{2,1,0:T(8,128)(2,1)} %bitcast.79), calls=%async_computation.11 | async-start | bytes 786432 | tf_op jit(solution)/shard_map/all_to_all | solution.py:253
  (112 other events, 1327.3 us)
Sparse Core Ops, SparseCore 0:
  10.8 63.0 all-gather.7
  80.0 62.4 all-gather.9
  145.3 52.7 all-gather.11
  200.9 58.0 all-gather.13
  261.6 57.8 all-gather.15
  322.3 57.8 all-gather.17
  506.8 34.1 reduce-scatter.9
  543.2 34.2 reduce-scatter.11
  596.2 62.4 all-gather.19
  838.7 33.9 reduce-scatter.13
  875.0 34.2 reduce-scatter.15
  915.0 100.9 reduce-scatter.19
  1023.2 113.6 reduce-scatter.21
  1143.0 113.7 reduce-scatter.23
  1263.7 113.7 reduce-scatter.25
  1383.6 118.2 reduce-scatter.17
where the time goes:
time: 1520 us; the launch traced here: 1510 us
  waiting for transfers between devices  881 us (58%)
  matrix products  331 us (22%)
  local copies, waits for them, and re-layouts  114 us (8%)
  blocking collectives  92.2 us (6%)
  other arithmetic  40.3 us (3%)
  starting transfers between devices  34.4 us (2%)
    reduce_scatter x1, waiting for transfers between devices, per_device(): lax.psum_scatter(grad_terms[1], ('dp', 'ctx'), scatter_dimension=0, tiled...  124 us
    reduce_scatter x1, waiting for transfers between devices, per_device(): lax.psum_scatter(grad_terms[4], ('dp', 'ctx'), scatter_dimension=0, tiled...  121 us
    reduce_scatter x1, waiting for transfers between devices, per_device(): lax.psum_scatter(grad_terms[6], ('dp', 'ctx'), scatter_dimension=0, tiled...  121 us
    reduce_scatter x1, waiting for transfers between devices, per_device(): lax.psum_scatter(grad_terms[5], ('dp', 'ctx'), scatter_dimension=0, tiled...  120 us
    all_gather x2, waiting for transfers between devices, per_device(): gathered = lax.all_gather(key_value, 'ctx', axis=0, tiled=True)  109 us
    unnamed x2, blocking collectives  82.2 us
    reduce_scatter x2, waiting for transfers between devices, per_device(): lax.psum_scatter(join_heads(grad_v_heads).astype(jnp.bfloat16), 'ctx', sc...  66.5 us
    all_gather x1, waiting for transfers between devices, per_device(): lax.all_gather(shards[4], ('dp', 'ctx'), axis=0, tiled=True)  57.9 us
  transfers between devices with their start and end apart: 23, of which 19 were waited for; matrix products, arithmetic and copies ran while one was open for 14% of the time, Pallas kernels for 0%

commit v1 on v0

v1 whole, which is shorter than its diff:
```python
import functools

import jax
import jax.numpy as jnp
from jax import lax
from jax.experimental import pallas as pl
from jax.experimental.pallas import tpu as pltpu
from jax.sharding import PartitionSpec as P

HEADS = 12
BLK = 256
SLOTS = 8
eps_norm = 1e-05
rope_base = 10000.0
MESH = pl.DeviceIdType.MESH
F32, BF16 = jnp.float32, jnp.bfloat16
NT = (((1,), (1,)), ((), ()))
TN = (((0,), (0,)), ((), ()))
ANY = pl.BlockSpec(memory_space=pl.ANY)
VM = pl.BlockSpec(memory_space=pltpu.VMEM)
SM = pl.BlockSpec(memory_space=pltpu.SMEM)


class Place:
    def __init__(self, ndp, nctx):
        self.ndp, self.nctx = ndp, nctx
        self.nb = 2
        self.na = ndp // 4
        self.g = nctx // 2
        self.gz = nctx // 4
        self.dp = lax.axis_index("dp")
        self.ctx = lax.axis_index("ctx")
        self.k, self.core = self.dp // 2, self.dp % 2
        self.ya, self.xb = self.k // self.nb, self.k % self.nb
        self.me = self.dp * nctx + self.ctx
        self.pack = self.ctx // self.gz
        self.j = self.core * self.gz + self.ctx % self.gz

    def member(self, j):
        return (self.k * 2 + j // self.gz, self.pack * self.gz + j % self.gz)

    def holder(self, m, d, c):
        j = jnp.where(c < self.g, c, 2 * self.g - 1 - c)
        return ((d // 2) * 2 + j // self.gz, (m * 2 + d % 2) * self.gz + j % self.gz)

    def dp_of(self, ya, xb, core):
        return (ya * self.nb + xb) * 2 + core


def entry_barrier(pc):
    total = pc.ndp * pc.nctx
    barrier = pltpu.get_barrier_semaphore()

    def greet(i, carry):
        other = (pc.me + i) % total
        pl.semaphore_signal(
            barrier, inc=1, device_id=(other // pc.nctx, other % pc.nctx), device_id_type=MESH
        )
        return carry

    lax.fori_loop(1, total, greet, 0)
    pl.semaphore_wait(barrier, total - 1)


def remote(src, dst, ss, rs, dev):
    return pltpu.make_async_remote_copy(
        src_ref=src, dst_ref=dst, send_sem=ss, recv_sem=rs, device_id=dev, device_id_type=MESH
    )


def gather_kernel(ndp, nctx, nt, x_ref, dy_ref, order_ref, len_ref, *refs):
    shards = refs[:nt]
    gx_ref, gdy_ref, plen_ref = refs[nt : nt + 3]
    full = refs[nt + 3 : nt + 3 + nt]
    (
        perm, tok_ss, tok_rs, len_ss, len_rs, own_sem,
        z_ss, z_rs, x_ss, x_rs, y_ss, y_rs, fa_ss, fa_rs, fb_ss, fb_rs, c_ss, c_rs,
    ) = refs[nt + 3 + nt :]
    pc = Place(ndp, nctx)
    na, nb = pc.na, pc.nb
    slot = BLK // ndp
    entry_barrier(pc)

    def block(t, dp, part=None):
        if part is None:
            return full[t].at[pl.ds(dp * nctx, nctx)]
        return full[t].at[pl.ds(dp * nctx + part * (nctx // 2), nctx // 2)]

    pending = []

    def z_copies(t):
        out = []
        for d in range(1, nctx):
            out.append(
                remote(
                    shards[t],
                    full[t].at[pc.me],
                    z_ss.at[t, d - 1],
                    z_rs.at[t, d - 1],
                    (pc.dp, (pc.ctx + d) % nctx),
                )
            )
        return out

    def own_copy(t):
        return pltpu.make_async_copy(shards[t], full[t].at[pc.me], own_sem.at[t])

    def x_copies(t):
        return [
            remote(
                block(t, pc.dp), block(t, pc.dp), x_ss.at[t, d - 1], x_rs.at[t, d - 1],
                (pc.dp_of(pc.ya, (pc.xb + d) % nb, pc.core), pc.ctx),
            )
            for d in range(1, nb)
        ]

    def y_copies(t):
        return [
            remote(
                block(t, pc.dp), block(t, pc.dp), y_ss.at[t, d - 1], y_rs.at[t, d - 1],
                (pc.dp_of((pc.ya + d) % na, pc.xb, pc.core), pc.ctx),
            )
            for d in range(1, na)
        ]

    def forward_copies(t):
        out = []
        for dx in range(1, nb):
            for dy in range(1, na):
                src = pc.dp_of(pc.ya, (pc.xb + nb - dx) % nb, pc.core)
                out.append(
                    remote(
                        block(t, src, 0), block(t, src, 0),
                        fa_ss.at[t, dx - 1, dy - 1], fa_rs.at[t, dx - 1, dy - 1],
                        (pc.dp_of((pc.ya + dy) % na, pc.xb, pc.core), pc.ctx),
                    )
                )
                src = pc.dp_of((pc.ya + na - dy) % na, pc.xb, pc.core)
                out.append(
                    remote(
                        block(t, src, 1), block(t, src, 1),
                        fb_ss.at[t, dx - 1, dy - 1], fb_rs.at[t, dx - 1, dy - 1],
                        (pc.dp_of(pc.ya, (pc.xb + dx) % nb, pc.core), pc.ctx),
                    )
                )
        return out

    def core_copy(t, dy, dx):
        src = pc.dp_of((pc.ya + na - dy) % na, (pc.xb + nb - dx) % nb, pc.core)
        return remote(
            block(t, src), block(t, src), c_ss.at[t, dy, dx], c_rs.at[t, dy, dx],
            (pc.k * 2 + 1 - pc.core, pc.ctx),
        )

    def start(copies):
        for cp in copies:
            cp.start()
            pending.append(cp)

    def token_copies(t, m, d):
        dp_to, ctx_to = pc.holder(m, d, pc.ctx)
        half = jnp.where(pc.ctx < pc.g, 0, 1)
        src = perm.at[t, m, pl.ds(pl.multiple_of(d * slot, slot), slot)]
        dst = (gx_ref, gdy_ref)[t].at[
            pl.ds(pl.multiple_of(half * BLK + pc.dp * slot, slot), slot)
        ]
        rs = tok_rs.at[t, half, pc.dp]
        same = (dp_to == pc.dp) & (ctx_to == pc.ctx)
        return (
            same,
            pltpu.make_async_copy(src, dst, rs),
            remote(src, dst, tok_ss.at[t, m, d], rs, (dp_to, ctx_to)),
        )

    def send_tokens(t, source):
        for m in range(2):
            order = order_ref[m]
            hot = (lax.broadcasted_iota(jnp.int32, (BLK, BLK), 1) == order).astype(BF16)
            perm[t, m] = jnp.dot(hot, source[m], preferred_element_type=F32).astype(BF16)

            def one(d, carry):
                same, near, far = token_copies(t, m, d)

                @pl.when(same)
                def _():
                    near.start()

                @pl.when(jnp.logical_not(same))
                def _():
                    far.start()

                return carry

            lax.fori_loop(0, ndp, one, 0)

    for t in range(nt):
        own_copy(t).start()
    start(z_copies(0))
    send_tokens(0, x_ref)
    len_copy = remote(len_ref, plen_ref, len_ss, len_rs, (pc.k * 2 + 1 - pc.core, pc.ctx))
    len_copy.start()
    start(z_copies(1))

    def got_xy(t):
        for cp in x_copies(t) + y_copies(t):
            cp.wait_recv()
        start(forward_copies(t))
        start([core_copy(t, 0, dx) for dx in range(1, nb)])
        start([core_copy(t, dy, 0) for dy in range(1, na)])

    def got_forward(t):
        for cp in forward_copies(t):
            cp.wait_recv()
        start([core_copy(t, dy, dx) for dy in range(1, na) for dx in range(1, nb)])

    for t in range(nt + 2):
        if t < nt:
            own_copy(t).wait()
            for cp in z_copies(t):
                cp.wait_recv()
            start(x_copies(t) + y_copies(t))
            start([core_copy(t, 0, 0)])
            if t + 2 < nt:
                start(z_copies(t + 2))
            if t + 2 == nt:
                send_tokens(1, dy_ref)
        if 1 <= t <= nt:
            got_xy(t - 1)
        if t >= 2:
            got_forward(t - 2)

    for t in range(nt):
        for dy in range(na):
            for dx in range(nb):
                core_copy(t, dy, dx).wait_recv()
    for cp in pending:
        cp.wait_send()
    len_copy.wait()
    for t in range(2):
        for m in range(2):

            def sent(d, carry):
                same, _near, far = token_copies(t, m, d)

                @pl.when(jnp.logical_not(same))
                def _():
                    far.wait_send()

                return carry

            lax.fori_loop(0, ndp, sent, 0)
        for half in range(2):

            def arrived(b, carry):
                dst = (gx_ref, gdy_ref)[t].at[
                    pl.ds(pl.multiple_of(half * BLK + b * slot, slot), slot)
                ]
                pltpu.make_async_copy(dst, dst, tok_rs.at[t, half, b]).wait()
                return carry

            lax.fori_loop(0, ndp, arrived, 0)


def gather_all(ndp, nctx, x, dy, order, lens, shards):
    nt = len(shards)
    n_all = ndp * nctx
    na, nb = ndp // 4, 2
    width = x.shape[-1]
    dma = pltpu.SemaphoreType.DMA
    return pl.pallas_call(
        functools.partial(gather_kernel, ndp, nctx, nt),
        out_shape=[
            jax.ShapeDtypeStruct((2 * BLK, width), BF16),
            jax.ShapeDtypeStruct((2 * BLK, width), BF16),
            jax.ShapeDtypeStruct(lens.shape, lens.dtype),
        ]
        + [jax.ShapeDtypeStruct((n_all,) + s.shape, s.dtype) for s in shards],
        in_specs=[VM, VM, VM, ANY] + [ANY] * nt,
        out_specs=[ANY] * (3 + nt),
        scratch_shapes=[
            pltpu.VMEM((2, 2, BLK, width), BF16),
            dma((2, 2, ndp)), dma((2, 2, ndp)), dma, dma, dma((nt,)),
            dma((nt, nctx - 1)), dma((nt, nctx - 1)),
            dma((nt, nb - 1)), dma((nt, nb - 1)),
            dma((nt, na - 1)), dma((nt, na - 1)),
            dma((nt, nb - 1, na - 1)), dma((nt, nb - 1, na - 1)),
            dma((nt, nb - 1, na - 1)), dma((nt, nb - 1, na - 1)),
            dma((nt, na, nb)), dma((nt, na, nb)),
        ],
        compiler_params=pltpu.CompilerParams(
            collective_id=0, has_side_effects=True, vmem_limit_bytes=32 << 20
        ),
        name="gather_all",
    )(x, dy, order, lens, *shards)


def scatter_kernel(ndp, nctx, nt, out_ref, gin_ref, order_ref, *refs):
    grads = refs[:nt]
    fin_out, fin_gin = refs[nt : nt + 2]
    shares = refs[nt + 2 : nt + 2 + nt]
    rest = refs[nt + 2 + nt :]
    from_core, diag_a, diag_b, from_x, from_y, own, zsend, zrecv = (
        rest[i * nt : (i + 1) * nt] for i in range(8)
    )
    h = nctx // 2
    (
        tok, tok_ss, tok_rs, c_ss, c_rs, da_ss, da_rs, db_ss, db_rs,
        x_ss, x_rs, y_ss, y_rs, z_ss, z_rs,
    ) = rest[8 * nt :]
    pc = Place(ndp, nctx)
    na, nb = pc.na, pc.nb
    slot = BLK // ndp
    entry_barrier(pc)
    pending = []

    def start(copies):
        for cp in copies:
            cp.start()
            pending.append(cp)

    def token_copies(t, half, b):
        c = jnp.where(half == 0, pc.j, 2 * pc.g - 1 - pc.j)
        d = pc.k * 2 + pc.pack % 2
        m = pc.pack // 2
        src = (out_ref, gin_ref)[t].at[
            pl.ds(pl.multiple_of(half * BLK + b * slot, slot), slot)
        ]
        dst = tok.at[t, m, pl.ds(pl.multiple_of(d * slot, slot), slot)]
        rs = tok_rs.at[t, m, d]
        same = (b == pc.dp) & (c == pc.ctx)
        return (
            same,
            pltpu.make_async_copy(src, dst, rs),
            remote(src, dst, tok_ss.at[t, half, b], rs, (b, c)),
        )

    def send_tokens(t):
        for half in range(2):

            def one(b, carry):
                same, near, far = token_copies(t, half, b)

                @pl.when(same)
                def _():
                    near.start()

                @pl.when(jnp.logical_not(same))
                def _():
                    far.start()

                return carry

            lax.fori_loop(0, ndp, one, 0)

    def place_tokens(t, fin):
        for half in range(2):

            def sent(b, carry):
                same, near, far = token_copies(t, half, b)

                @pl.when(jnp.logical_not(same))
                def _():
                    far.wait_send()

                return carry

            lax.fori_loop(0, ndp, sent, 0)
        for m in range(2):

            def arrived(d, carry):
                dst = tok.at[t, m, pl.ds(pl.multiple_of(d * slot, slot), slot)]
                pltpu.make_async_copy(dst, dst, tok_rs.at[t, m, d]).wait()
                return carry

            lax.fori_loop(0, ndp, arrived, 0)
            order = order_ref[m]
            hot = (lax.broadcasted_iota(jnp.int32, (BLK, BLK), 0) == order).astype(BF16)
            fin[m] = jnp.dot(hot, tok[t, m], preferred_element_type=F32).astype(BF16)

    def core_copy(t, dy, dx):
        k = ((pc.ya + dy) % na) * nb + (pc.xb + dx) % nb
        src = grads[t].at[pl.ds((k * 2 + 1 - pc.core) * nctx, nctx)]
        return remote(
            src, from_core[t].at[dy, dx], c_ss.at[t, dy, dx], c_rs.at[t, dy, dx],
            (pc.k * 2 + 1 - pc.core, pc.ctx),
        )

    def add_core(t, dy, dx):
        k = ((pc.ya + dy) % na) * nb + (pc.xb + dx) % nb
        mine = grads[t][pl.ds((k * 2 + pc.core) * nctx, nctx)].astype(F32)
        both = mine + from_core[t][dy, dx].astype(F32)
        if dy == 0 and dx == 0:
            own[t][...] = both
        else:
            from_core[t][dy, dx] = both.astype(BF16)

    def diag_copies(t):
        out = []
        for dy in range(1, na):
            for dx in range(1, nb):
                out.append(
                    remote(
                        from_core[t].at[dy, dx, pl.ds(0, h)], diag_a[t].at[dy - 1, dx - 1],
                        da_ss.at[t, dy - 1, dx - 1], da_rs.at[t, dy - 1, dx - 1],
                        (pc.dp_of((pc.ya + dy) % na, pc.xb, pc.core), pc.ctx),
                    )
                )
                out.append(
                    remote(
                        from_core[t].at[dy, dx, pl.ds(h, h)], diag_b[t].at[dy - 1, dx - 1],
                        db_ss.at[t, dy - 1, dx - 1], db_rs.at[t, dy - 1, dx - 1],
                        (pc.dp_of(pc.ya, (pc.xb + dx) % nb, pc.core), pc.ctx),
                    )
                )
        return out

    def add_diag(t):
        for dx in range(1, nb):
            part = from_core[t][0, dx, pl.ds(0, h)].astype(F32)
            for dy in range(1, na):
                part = part + diag_a[t][dy - 1, dx - 1].astype(F32)
            from_core[t][0, dx, pl.ds(0, h)] = part.astype(BF16)
        for dy in range(1, na):
            part = from_core[t][dy, 0, pl.ds(h, h)].astype(F32)
            for dx in range(1, nb):
                part = part + diag_b[t][dy - 1, dx - 1].astype(F32)
            from_core[t][dy, 0, pl.ds(h, h)] = part.astype(BF16)

    def xy_copies(t):
        out = []
        for dx in range(1, nb):
            out.append(
                remote(
                    from_core[t].at[0, dx], from_x[t].at[dx - 1],
                    x_ss.at[t, dx - 1], x_rs.at[t, dx - 1],
                    (pc.dp_of(pc.ya, (pc.xb + dx) % nb, pc.core), pc.ctx),
                )
            )
        for dy in range(1, na):
            out.append(
                remote(
                    from_core[t].at[dy, 0], from_y[t].at[dy - 1],
                    y_ss.at[t, dy - 1], y_rs.at[t, dy - 1],
                    (pc.dp_of((pc.ya + dy) % na, pc.xb, pc.core), pc.ctx),
                )
            )
        return out

    def add_xy(t):
        total = own[t][...]
        for i in range(nb - 1):
            total = total + from_x[t][i].astype(F32)
        for i in range(na - 1):
            total = total + from_y[t][i].astype(F32)
        own[t][...] = total
        zsend[t][...] = total.astype(BF16)

    def z_copies(t):
        return [
            remote(
                zsend[t].at[(pc.ctx + d) % nctx], zrecv[t].at[d - 1],
                z_ss.at[t, d - 1], z_rs.at[t, d - 1], (pc.dp, (pc.ctx + d) % nctx),
            )
            for d in range(1, nctx)
        ]

    def add_z(t):
        total = own[t][pc.ctx]
        for i in range(nctx - 1):
            total = total + zrecv[t][i].astype(F32)
        shares[t][...] = total

    order_yx = [(dy, dx) for dy in range(1, na) for dx in range(1, nb)]
    order_yx += [(0, dx) for dx in range(1, nb)] + [(dy, 0) for dy in range(1, na)] + [(0, 0)]

    send_tokens(0)
    for t in range(nt):
        start([core_copy(t, dy, dx) for dy, dx in order_yx])
    for t in range(nt + 3):
        if t < nt:
            for dy, dx in order_yx:
                core_copy(t, dy, dx).wait_recv()
                add_core(t, dy, dx)
            start(diag_copies(t))
        if 1 <= t <= nt:
            for cp in diag_copies(t - 1):
                cp.wait_recv()
            add_diag(t - 1)
            start(xy_copies(t - 1))
        if 2 <= t <= nt + 1:
            for cp in xy_copies(t - 2):
                cp.wait_recv()
            add_xy(t - 2)
            start(z_copies(t - 2))
        if t == 1:
            send_tokens(1)
        if t == 3:
            place_tokens(0, fin_out)
        if t >= 3:
            for cp in z_copies(t - 3):
                cp.wait_recv()
            add_z(t - 3)
    place_tokens(1, fin_gin)
    for cp in pending:
        cp.wait_send()


def scatter_all(ndp, nctx, out, gin, order, grads):
    nt = len(grads)
    na, nb = ndp // 4, 2
    width = out.shape[-1]
    dma = pltpu.SemaphoreType.DMA
    scratch = []
    spec = [g.shape[1:] for g in grads]
    scratch += [pltpu.VMEM((na, nb, nctx) + s, BF16) for s in spec]
    scratch += [pltpu.VMEM((na - 1, nb - 1, nctx // 2) + s, BF16) for s in spec]
    scratch += [pltpu.VMEM((na - 1, nb - 1, nctx // 2) + s, BF16) for s in spec]
    scratch += [pltpu.VMEM((nb - 1, nctx) + s, BF16) for s in spec]
    scratch += [pltpu.VMEM((na - 1, nctx) + s, BF16) for s in spec]
    scratch += [pltpu.VMEM((nctx,) + s, F32) for s in spec]
    scratch += [pltpu.VMEM((nctx,) + s, BF16) for s in spec]
    scratch += [pltpu.VMEM((nctx - 1,) + s, BF16) for s in spec]
    scratch += [
        pltpu.VMEM((2, 2, BLK, width), BF16),
        dma((2, 2, ndp)), dma((2, 2, ndp)),
        dma((nt, na, nb)), dma((nt, na, nb)),
        dma((nt, na - 1, nb - 1)), dma((nt, na - 1, nb - 1)),
        dma((nt, na - 1, nb - 1)), dma((nt, na - 1, nb - 1)),
        dma((nt, nb - 1)), dma((nt, nb - 1)),
        dma((nt, na - 1)), dma((nt, na - 1)),
        dma((nt, nctx - 1)), dma((nt, nctx - 1)),
    ]
    return pl.pallas_call(
        functools.partial(scatter_kernel, ndp, nctx, nt),
        out_shape=[jax.ShapeDtypeStruct((2, BLK, width), BF16)] * 2
        + [jax.ShapeDtypeStruct(s, F32) for s in spec],
        in_specs=[VM] * (3 + nt),
        out_specs=[VM] * (2 + nt),
        scratch_shapes=scratch,
        compiler_params=pltpu.CompilerParams(
            collective_id=1, has_side_effects=True, vmem_limit_bytes=60 << 20
        ),
        name="scatter_all",
    )(out, gin, order, *grads)


def group_barrier(pc):
    barrier = pltpu.get_barrier_semaphore()
    for o in range(1, pc.g):
        pl.semaphore_signal(
            barrier, inc=1, device_id=pc.member((pc.j + o) % pc.g), device_id_type=MESH
        )
    pl.semaphore_wait(barrier, pc.g - 1)


def block_at(ref, index, size=BLK):
    return ref.at[pl.ds(pl.multiple_of(index * size, size), size)]


def kv_kernel(ndp, nctx, kv_ref, all_ref, own_sem, ss, rs):
    pc = Place(ndp, nctx)
    group_barrier(pc)
    copies = []
    for half in range(2):
        where = pc.j if half == 0 else 2 * pc.g - 1 - pc.j
        src, dst = block_at(kv_ref, half), block_at(all_ref, where)
        for o in range(1, pc.g):
            copies.append(
                remote(src, dst, ss.at[half, o - 1], rs.at[half, o - 1], pc.member((pc.j + o) % pc.g))
            )
        copies.append(pltpu.make_async_copy(src, dst, own_sem.at[half]))
    for cp in copies:
        cp.start()
    for cp in copies:
        cp.wait()


def share_kv(ndp, nctx, kv):
    g = nctx // 2
    dma = pltpu.SemaphoreType.DMA
    return pl.pallas_call(
        functools.partial(kv_kernel, ndp, nctx),
        out_shape=jax.ShapeDtypeStruct((g * kv.shape[0], kv.shape[1]), kv.dtype),
        in_specs=[ANY],
        out_specs=ANY,
        scratch_shapes=[dma((2,)), dma((2, g - 1)), dma((2, g - 1))],
        compiler_params=pltpu.CompilerParams(
            collective_id=2, has_side_effects=True, vmem_limit_bytes=16 << 20
        ),
        name="share_kv",
    )(kv)


def dkv_kernel(ndp, nctx, part_ref, sum_ref, got, ss, rs):
    pc = Place(ndp, nctx)
    group_barrier(pc)
    copies = []
    for o in range(1, pc.g):
        to = (pc.j + o) % pc.g
        for half in range(2):
            where = to if half == 0 else 2 * pc.g - 1 - to
            copies.append(
                remote(
                    block_at(part_ref, where), got.at[o - 1, half],
                    ss.at[half, o - 1], rs.at[half, o - 1], pc.member(to),
                )
            )
    for cp in copies:
        cp.start()
    for cp in copies:
        cp.wait()
    for half in range(2):
        where = pc.j if half == 0 else 2 * pc.g - 1 - pc.j
        total = part_ref[pl.ds(pl.multiple_of(where * BLK, BLK), BLK)].astype(F32)
        for o in range(1, pc.g):
            total = total + got[o - 1, half].astype(F32)
        sum_ref[half * BLK : (half + 1) * BLK] = total


def sum_dkv(ndp, nctx, part):
    g = nctx // 2
    width = part.shape[1]
    dma = pltpu.SemaphoreType.DMA
    return pl.pallas_call(
        functools.partial(dkv_kernel, ndp, nctx),
        out_shape=jax.ShapeDtypeStruct((2 * BLK, width), F32),
        in_specs=[VM],
        out_specs=VM,
        scratch_shapes=[
            pltpu.VMEM((g - 1, 2, BLK, width), BF16), dma((2, g - 1)), dma((2, g - 1)),
        ],
        compiler_params=pltpu.CompilerParams(
            collective_id=3, has_side_effects=True, vmem_limit_bytes=32 << 20
        ),
        name="sum_dkv",
    )(part)


NEG = -1e30


def lane_mask(h):
    lanes = lax.broadcasted_iota(jnp.int32, (1, 128), 1)
    return (lanes < 64) if h == 0 else (lanes >= 64)


def fill_bias(qi, nk, blk, segk_ref, segq_ref, bias):
    segq = segq_ref[:, qi * BLK : (qi + 1) * BLK]
    qrow = blk * BLK + lax.broadcasted_iota(jnp.int32, (BLK, BLK), 1)

    def one(kb, carry):
        segk = segk_ref[pl.ds(pl.multiple_of(kb * BLK, BLK), BLK)]
        krow = kb * BLK + lax.broadcasted_iota(jnp.int32, (BLK, BLK), 0)
        bias[kb] = jnp.where((segk == segq) & (krow <= qrow), 0.0, NEG)
        return carry

    lax.fori_loop(0, nk, one, 0)


def tile(ref, kb, col):
    return ref[pl.ds(pl.multiple_of(kb * BLK, BLK), BLK), pl.ds(pl.multiple_of(col, 128), 128)]


def attend_kernel(blk_ref, q_ref, kv_ref, segk_ref, segq_ref, o_ref, lse_ref, bias, sbuf):
    width = q_ref.shape[1]
    for qi in range(2):
        blk = blk_ref[qi]
        nk = blk + 1
        fill_bias(qi, nk, blk, segk_ref, segq_ref, bias)

        def pair(hp, carry):
            qp = q_ref[qi * BLK : (qi + 1) * BLK, pl.ds(pl.multiple_of(hp * 128, 128), 128)]
            outs = []
            for h in range(2):
                qm = jnp.where(lane_mask(h), qp, 0) * 0.125
                qm = qm.astype(BF16)

                def score(kb, top):
                    s = lax.dot_general(
                        tile(kv_ref, kb, hp * 128), qm, NT, preferred_element_type=F32
                    )
                    s = s + bias[kb]
                    sbuf[kb] = s
                    return jnp.maximum(top, jnp.max(s, axis=0, keepdims=True))

                top = lax.fori_loop(0, nk, score, jnp.full((1, BLK), NEG, F32))

                def expo(kb, total):
                    p = jnp.exp(sbuf[kb] - top)
                    sbuf[kb] = p
                    return total + jnp.sum(p, axis=0, keepdims=True)

                total = lax.fori_loop(0, nk, expo, jnp.zeros((1, BLK), F32))
                inv = 1.0 / total

                def mix(kb, acc):
                    p = (sbuf[kb] * inv).astype(BF16)
                    return acc + lax.dot_general(
                        tile(kv_ref, kb, width + hp * 128), p, TN, preferred_element_type=F32
                    )

                acc = lax.fori_loop(0, nk, mix, jnp.zeros((128, BLK), F32))
                outs.append(acc)
                lse_ref[hp, h : h + 1, qi * BLK : (qi + 1) * BLK] = top + jnp.log(total)
            sub = lax.broadcasted_iota(jnp.int32, (128, BLK), 0)
            o = jnp.where(sub < 64, outs[0], outs[1])
            o_ref[qi * BLK : (qi + 1) * BLK, pl.ds(pl.multiple_of(hp * 128, 128), 128)] = (
                o.T.astype(BF16)
            )
            return carry

        lax.fori_loop(0, HEADS // 2, pair, 0)


def attend(blk, q, kv, segk, segq):
    group, width = kv.shape[0], q.shape[1]
    nb = group // BLK
    return pl.pallas_call(
        attend_kernel,
        out_shape=[
            jax.ShapeDtypeStruct((2 * BLK, width), BF16),
            jax.ShapeDtypeStruct((HEADS // 2, 2, 2 * BLK), F32),
        ],
        in_specs=[SM, VM, VM, VM, VM],
        out_specs=[VM, VM],
        scratch_shapes=[pltpu.VMEM((nb, BLK, BLK), F32), pltpu.VMEM((nb, BLK, BLK), F32)],
        compiler_params=pltpu.CompilerParams(vmem_limit_bytes=48 << 20),
        name="attend",
    )(blk, q, kv, segk, segq)


def attend_back_kernel(
    blk_ref, q_ref, kv_ref, do_ref, lse_ref, segk_ref, segq_ref, dq_ref, dkv_ref,
    bias, pbuf, dpbuf, dkv_acc,
):
    width = q_ref.shape[1]
    dkv_acc[...] = jnp.zeros_like(dkv_acc)
    for qi in range(2):
        blk = blk_ref[qi]
        nk = blk + 1
        fill_bias(qi, nk, blk, segk_ref, segq_ref, bias)
        rows = slice(qi * BLK, (qi + 1) * BLK)

        def pair(hp, carry):
            cols = pl.ds(pl.multiple_of(hp * 128, 128), 128)
            qp, dop = q_ref[rows, cols], do_ref[rows, cols]
            dqs = []
            for h in range(2):
                qm = (jnp.where(lane_mask(h), qp, 0) * 0.125).astype(BF16)
                dom = jnp.where(lane_mask(h), dop, 0).astype(BF16)
                lse = lse_ref[hp, h : h + 1, rows]

                def first(kb, weighted):
                    s = lax.dot_general(
                        tile(kv_ref, kb, hp * 128), qm, NT, preferred_element_type=F32
                    )
                    p = jnp.exp(s + bias[kb] - lse)
                    dp = lax.dot_general(
                        tile(kv_ref, kb, width + hp * 128), dom, NT, preferred_element_type=F32
                    )
                    pbuf[kb] = p
                    dpbuf[kb] = dp
                    return weighted + jnp.sum(p * dp, axis=0, keepdims=True)

                weighted = lax.fori_loop(0, nk, first, jnp.zeros((1, BLK), F32))

                def second(kb, acc):
                    p = pbuf[kb]
                    ds = (p * (dpbuf[kb] - weighted)).astype(BF16)
                    krows = pl.ds(pl.multiple_of(kb * BLK, BLK), BLK)
                    dkv_acc[krows, cols] += jnp.dot(ds, qm, preferred_element_type=F32)
                    vcols = pl.ds(pl.multiple_of(width + hp * 128, 128), 128)
                    dkv_acc[krows, vcols] += jnp.dot(
                        p.astype(BF16), dom, preferred_element_type=F32
                    )
                    return acc + lax.dot_general(
                        tile(kv_ref, kb, hp * 128), ds, TN, preferred_element_type=F32
                    )

                dqs.append(lax.fori_loop(0, nk, second, jnp.zeros((128, BLK), F32)))
            sub = lax.broadcasted_iota(jnp.int32, (128, BLK), 0)
            dq = jnp.where(sub < 64, dqs[0], dqs[1]) * 0.125
            dq_ref[rows, cols] = dq.T
            return carry

        lax.fori_loop(0, HEADS // 2, pair, 0)
    dkv_ref[...] = dkv_acc[...].astype(BF16)


def attend_back(blk, q, kv, do, lse, segk, segq):
    group, width = kv.shape[0], q.shape[1]
    nb = group // BLK
    return pl.pallas_call(
        attend_back_kernel,
        out_shape=[
            jax.ShapeDtypeStruct((2 * BLK, width), F32),
            jax.ShapeDtypeStruct((group, 2 * width), BF16),
        ],
        in_specs=[SM] + [VM] * 6,
        out_specs=[VM, VM],
        scratch_shapes=[pltpu.VMEM((nb, BLK, BLK), F32)] * 3
        + [pltpu.VMEM((group, 2 * width), F32)],
        compiler_params=pltpu.CompilerParams(vmem_limit_bytes=56 << 20),
        name="attend_back",
    )(blk, q, kv, do, lse, segk, segq)


def inverse_rms(values):
    return lax.rsqrt(jnp.mean(values * values, axis=-1, keepdims=True) + eps_norm)


def norm_back(grad, values, inverse, gain):
    scaled = grad * gain
    mean = jnp.mean(scaled * values, axis=-1, keepdims=True)
    return (
        inverse * scaled - values * (inverse * inverse * inverse) * mean,
        jnp.sum(grad * values * inverse, axis=0),
    )


def swap_halves(values):
    lane = lax.broadcasted_iota(jnp.int32, values.shape, 1) % 64
    return jnp.where(lane < 32, jnp.roll(values, -32, axis=1), jnp.roll(values, 32, axis=1))


def dot(a, b):
    return jnp.dot(a, b, preferred_element_type=F32)


def dot_nt(a, b):
    return lax.dot_general(a, b, NT, preferred_element_type=F32)


def dot_tn(a, b):
    return lax.dot_general(a, b, TN, preferred_element_type=F32)


def per_device(
    inputs, cotangent, lengths, send_order,
    norm1_gain, qkv_weight, out_weight, norm2_gain, gate_weight, up_weight, down_weight,
):
    ndp, nctx = lax.axis_size("dp"), lax.axis_size("ctx")
    n_all = ndp * nctx
    width = inputs.shape[2]
    head = width // HEADS
    pc = Place(ndp, nctx)
    share = norm1_gain.shape[0]
    pad = jnp.zeros((SLOTS, 128), BF16).at[0, :share].set(norm1_gain).at[1, :share].set(norm2_gain)
    lens = jnp.zeros((8, 128), jnp.int32).at[:2, : lengths.shape[2]].set(lengths[:, 0])
    order_row = send_order
    order_col = jnp.swapaxes(send_order, 1, 2)
    x, dy, partner_lens, wqkv, wout, gains, wgate, wup, wdown = gather_all(
        ndp, nctx, inputs, cotangent, order_col, lens,
        [qkv_weight, out_weight, pad, gate_weight, up_weight, down_weight],
    )
    wqkv, wout, wgate, wup, wdown = (
        w.reshape(-1, w.shape[2]) for w in (wqkv, wout, wgate, wup, wdown)
    )
    gain1 = gains[:, 0, :share].reshape(1, width).astype(F32)
    gain2 = gains[:, 1, :share].reshape(1, width).astype(F32)

    both = jnp.where(pc.pack % 2 == pc.core, lens, partner_lens)
    seq_lengths = lax.dynamic_index_in_dim(both, pc.pack // 2, 0, keepdims=False)[: lengths.shape[2]]
    blocks = jnp.stack([pc.j, 2 * pc.g - 1 - pc.j]).astype(jnp.int32)
    rows = (blocks[:, None] * BLK + jnp.arange(BLK, dtype=jnp.int32)[None, :]).reshape(-1)
    ends = jnp.cumsum(seq_lengths)
    passed = (rows[:, None] >= ends[None, :]).astype(jnp.int32)
    segq = jnp.sum(passed, axis=1)
    position = rows - jnp.sum(passed * seq_lengths[None, :], axis=1)
    key_rows = jnp.arange(pc.g * 2 * BLK, dtype=jnp.int32)
    segk = jnp.sum((key_rows[:, None] >= ends[None, :]).astype(jnp.int32), axis=1)
    segq, segk = segq[None, :], segk[:, None]
    half = head // 2
    frequency = rope_base ** (-(jnp.arange(half, dtype=F32) * 2.0 / head))
    angles = position.astype(F32)[:, None] * frequency[None, :]
    cosine, sine = jnp.cos(angles), jnp.sin(angles)
    cos_all = jnp.tile(jnp.concatenate([cosine, cosine], 1), (1, HEADS))
    sin_all = jnp.tile(jnp.concatenate([-sine, sine], 1), (1, HEADS))

    xin, grad_out = x.astype(F32), dy.astype(F32)
    r1 = inverse_rms(xin)
    normed1 = (xin * r1 * gain1).astype(BF16)
    qkv = dot(normed1, wqkv)
    q_raw, k_raw = qkv[:, :width], qkv[:, width : 2 * width]
    queries = (q_raw * cos_all + swap_halves(q_raw) * sin_all).astype(BF16)
    keys = (k_raw * cos_all + swap_halves(k_raw) * sin_all).astype(BF16)
    kv = jnp.concatenate([keys, qkv[:, 2 * width :].astype(BF16)], axis=1)
    kv_all = share_kv(ndp, nctx, kv)
    attended, lse = attend(blocks, queries, kv_all, segk, segq)
    hidden = xin + dot(attended, wout)
    r2 = inverse_rms(hidden)
    normed2 = (hidden * r2 * gain2).astype(BF16)
    gate, up = dot(normed2, wgate), dot(normed2, wup)
    sig = 1.0 / (1.0 + jnp.exp(-gate))
    act = gate * sig
    inner = (act * up).astype(BF16)
    layer_out = (hidden + dot(inner, wdown)).astype(BF16)

    d_down = dot_tn(inner, dy).astype(BF16)
    grad_inner = dot_nt(dy, wdown)
    g_gate = (grad_inner * up * (sig * (1.0 + gate * (1.0 - sig)))).astype(BF16)
    g_up = (grad_inner * act).astype(BF16)
    d_gate = dot_tn(normed2, g_gate).astype(BF16)
    d_up = dot_tn(normed2, g_up).astype(BF16)
    grad_normed2 = dot_nt(g_gate, wgate) + dot_nt(g_up, wup)
    grad_hidden, d_gain2 = norm_back(grad_normed2, hidden, r2, gain2)
    grad_hidden = grad_out + grad_hidden
    g_branch = grad_hidden.astype(BF16)
    d_out = dot_tn(attended, g_branch).astype(BF16)
    grad_attended = dot_nt(g_branch, wout).astype(BF16)
    dq, dkv_part = attend_back(blocks, queries, kv_all, grad_attended, lse, segk, segq)
    dkv = sum_dkv(ndp, nctx, dkv_part)
    dk = dkv[:, :width]
    grad_qkv = jnp.concatenate(
        [
            dq * cos_all - swap_halves(dq) * sin_all,
            dk * cos_all - swap_halves(dk) * sin_all,
            dkv[:, width:],
        ],
        axis=1,
    ).astype(BF16)
    d_qkv = dot_tn(normed1, grad_qkv).astype(BF16)
    grad_normed1 = dot_nt(grad_qkv, wqkv)
    grad_x, d_gain1 = norm_back(grad_normed1, xin, r1, gain1)
    input_grad = (grad_hidden + grad_x).astype(BF16)

    d_gains = jnp.zeros((n_all, SLOTS, 128), BF16)
    d_gains = d_gains.at[:, 0, :share].set(d_gain1.reshape(n_all, share).astype(BF16))
    d_gains = d_gains.at[:, 1, :share].set(d_gain2.reshape(n_all, share).astype(BF16))
    fin_out, fin_gin, s_down, s_gate, s_up, s_out, s_qkv, s_gains = scatter_all(
        ndp, nctx, layer_out, input_grad, order_row,
        [d.reshape(n_all, -1, d.shape[1]) for d in (d_down, d_gate, d_up, d_out, d_qkv)] + [d_gains],
    )
    return (
        fin_out, fin_gin, s_gains[0, :share], s_qkv, s_out, s_gains[1, :share],
        s_gate, s_up, s_down,
    )


def solution(mesh):
    both = ("dp", "ctx")
    in_specs = (
        P(None, both, None), P(None, both, None), P(None, "dp", None), P(None, both, None),
        P(both), P(both, None), P(both, None), P(both), P(both, None), P(both, None), P(both, None),
    )
    out_specs = (
        P(None, both, None), P(None, both, None),
        P(both), P(both, None), P(both, None), P(both), P(both, None), P(both, None), P(both, None),
    )
    return jax.shard_map(
        per_device, mesh=mesh, in_specs=in_specs, out_specs=out_specs, check_vma=False
    )
```

time: 1520 us -> 388 us (0.26)
  waiting for transfers between devices: 881 us -> 0 us
  matrix products: 331 us -> 44.7 us
  Pallas kernels: 0 us -> 278 us
  blocking collectives: 92.2 us -> 0 us
  local copies, waits for them, and re-layouts: 114 us -> 46.3 us
  starting transfers between devices: 34.4 us -> 0 us
  other arithmetic: 40.3 us -> 9.69 us
    reduce_scatter x9 -> x0, waiting for transfers between devices: 576 us -> none  [the longest x1 124 us: per_device(): lax.psum_scatter(grad_terms[1], ('dp', 'ctx'), scatter_dimension=0, tiled...]
    all_gather x7 -> x0, waiting for transfers between devices: 291 us -> none  [the longest x2 109 us: per_device(): gathered = lax.all_gather(key_value, 'ctx', axis=0, tiled=True)]
    dot_general x198 -> x15, matrix products: 331 us -> 44.7 us  [the longest x5 18.3 us: dot_tn(): return lax.dot_general(a, b, TN, preferred_element_type=F32)]
    pallas_call x0 -> x6, Pallas kernels: none -> 278 us  [the longest x1 105 us: scatter_all(): pl.pallas_call(functools.partial(scatter_kernel, ndp, nctx, nt), out_shap...]
    unnamed x2 -> x0, blocking collectives: 82.2 us -> none
    all_to_all x7 -> x0, starting transfers between devices: 32.9 us -> none  [the longest x2 10.3 us: per_device(): lax.all_to_all(grad_input.reshape(peer_count, slot_rows, model_width), 'd...]
    slice x15 -> x8, local copies, waits for them, and re-layouts: 25 us -> 2.65 us  [the longest x6 2.48 us: swap_halves(): jnp.roll(values, 32, axis=1)]
    dynamic_slice x24 -> x1, local copies, waits for them, and re-layouts: 16.7 us -> 0.01 us  [per_device(): lax.dynamic_index_in_dim(both, pc.pack // 2, 0, keepdims=False)]
  transfers between devices with their start and end apart: 23 -> 0, of which waited for: 19 -> 0; matrix products, arithmetic and copies ran while one was open for 14% -> 0% of each run, Pallas kernels for 0% -> 0%
where the time goes in v1:
time: 388 us; the launch traced here: 381 us
  Pallas kernels  278 us (72%)
  local copies, waits for them, and re-layouts  46.3 us (12%)
  matrix products  44.7 us (12%)
  other arithmetic  9.69 us (2%)
    pallas_call x1, Pallas kernels, scatter_all(): pl.pallas_call(functools.partial(scatter_kernel, ndp, nctx, nt), out_shap...  105 us
    pallas_call x1, Pallas kernels, gather_all(): pl.pallas_call(functools.partial(gather_kernel, ndp, nctx, nt), out_shape...  98 us
    pallas_call x1, Pallas kernels, attend_back(): pl.pallas_call(attend_back_kernel, out_shape=[jax.ShapeDtypeStruct((2 * B...  37.5 us
    pallas_call x1, Pallas kernels, attend(): pl.pallas_call(attend_kernel, out_shape=[jax.ShapeDtypeStruct((2 * BLK, w...  30.4 us
    unnamed x128, local copies, waits for them, and re-layouts  28.7 us
    dot_general x5, matrix products, dot_tn(): return lax.dot_general(a, b, TN, preferred_element_type=F32)  18.3 us
    dot_general x5, matrix products, dot(): return jnp.dot(a, b, preferred_element_type=F32)  13.6 us
    dot_general x5, matrix products, dot_nt(): return lax.dot_general(a, b, NT, preferred_element_type=F32)  12.8 us

profile of v1, /device:TPU:4, one launch (start us, length us, event | category | flops | bytes accessed | tf_op | source)
XLA Modules:
  0.0 380.9 jit_solution(6312299115708772263)
XLA Ops:
  11.6 98.0 %gather_all.1 = (bf16[512,768]{1,0:T(8,128)(2,1)S(1)}, bf16[512,768]{1,0:T(8,128)(2,1)S(1)}, s32[8,128]{1,0:T(8,128)S(1)}, bf16[32,24,2304]{2,1,0:T(8,128)(2,1)S...) custom-call(bf16[2,256,768]{2,1,0:T(8,128)(2,1)S(1)} %copy-done.10, ...), custom_call_target="tpu_custom_call" | custom-call | tf_op jit(solution)/shard_map/gather_all/pallas_call | solution.py:270
  109.6 1.7 copy-done.20
  121.7 3.1 copy.34
  126.1 3.1 copy.35
  129.2 4.1 %fusion.27 = f32[512,2304]{1,0:T(8,128)S(1)} fusion(bf16[768,2304]{1,0:T(8,128)(2,1)} %bitcast.57, bf16[512,768]{1,0:T(8,128)(2,1)S(1)} %get-tuple-element.90, f32[768]{0:T(1024)S(1)} %copy-done.51, f32[512]{0:T(512)S(1)} %copy-done.52), kind=kOutput, calls=%fused_computation.60 | convolution fusion | flops 1813512192 | bytes 9049088 | tf_op jit(solution)/shard_map/dot_general | solution.py:827
  137.3 3.7 share_kv.1.kv_ref
  141.1 30.4 %attend.1 = (bf16[512,768]{1,0:T(8,128)(2,1)S(1)}, f32[6,2,512]{2,1,0:T(2,128)S(1)}) custom-call(s32[2]{0:T(128)S(1)} %get-tuple-element.120.blk_ref, bf16[512,768]{1,0:T(8,128)(2,1)S(1)} %get-tuple-element.125.q_ref, bf16[1024,1536]{1,0:T(8,128)(2,1)S(1)} %share_kv.1.kv_ref, s32[1024,1]{1,0:T(8,128)S(1)} %copy.38.segk_ref, s32[1,512]{1,0:T(1,128)S(1)} %bitcast.55), custom_call_target="tpu_custom_call" | custom-call | tf_op jit(solution)/shard_map/attend/pallas_call | solution.py:718
  173.8 1.8 fusion.45
  175.9 1.8 fusion.44
  177.8 4.8 %multiply_convert_fusion = (bf16[512,2048]{1,0:T(8,128)(2,1)S(1)}, bf16[512,2048]{1,0:T(8,128)(2,1)}, bf16[512,2048]{1,0:T(8,128)(2,1)}) fusion(f32[512,2048]{1,0:T(8,128)S(1)} %fusion.44, f32[512,2048]{1,0:T(8,128)S(1)} %fusion.45, bf16[512,768]{1,0:T(8,128)(2,1)S(1)} %get-tuple-element.99, bf16[2048,768]{1,0:T(8,128)(2,1)S(1)} %bitcast.63), kind=kOutput, calls=%fused_computation.1 | convolution fusion | flops 1626341376 | bytes 18612224 | tf_op jit(solution)/shard_map/dot_general | solution.py:831
  182.6 5.1 %add_convert_fusion.out_ref = bf16[512,768]{1,0:T(8,128)(2,1)} fusion(f32[512,768]{1,0:T(8,128)S(1)} %get-tuple-element.156, bf16[512,2048]{1,0:T(8,128)(2,1)} %get-tuple-element.123, bf16[2048,768]{1,0:T(8,128)(2,1)S(1)} %bitcast.64), kind=kOutput, calls=%fused_computation.50 | convolution fusion | flops 1611399168 | bytes 7602176 | tf_op jit(solution)/shard_map/dot_general | solution.py:827
  187.7 1.9 fusion.46
  189.6 2.1 multiply_reduce_fusion
  195.1 37.5 %attend_back.1 = (f32[512,768]{1,0:T(8,128)}, bf16[1024,1536]{1,0:T(8,128)(2,1)}) custom-call(s32[2]{0:T(128)} %copy-done.19, bf16[512,768]{1,0:T(8,128)(2,1)} %copy-done.1, bf16[1024,1536]{1,0:T(8,128)(2,1)} %copy-done, bf16[512,768]{1,0:T(8,128)(2,1)} %convolution_convert_fusion.5.do_ref, f32[6,2,512]{2,1,0:T(2,128)} %copy-done.17, s32[1024,1]{1,0:T(8,128)} %copy-done.2, ...), custom_call_target="tpu_custom_call" | custom-call | tf_op jit(solution)/shard_map/attend_back/pallas_call | solution.py:793
  232.6 1.9 copy-done.3
  234.5 3.8 sum_dkv.1
  238.4 5.4 %convolution_convert_fusion.3 = bf16[2048,768]{1,0:T(8,128)(2,1)} fusion(bf16[512,2048]{1,0:T(8,128)(2,1)} %get-tuple-element.123, bf16[512,768]{1,0:T(8,128)(2,1)} %copy-done.7), kind=kOutput, calls=%fused_computation.14 | convolution fusion | flops 1612185600 | bytes 6029312 | tf_op jit(solution)/shard_map/dot_general | solution.py:835
  243.8 1.8 convolution_convert_fusion.4
  247.4 3.5 convolution_convert_fusion.1
  251.0 3.6 convolution_convert_fusion.2
  259.2 2.2 fusion.10
  263.9 3.9 %convolution_convert_fusion = bf16[768,2304]{1,0:T(8,128)(2,1)} fusion(bf16[512,768]{1,0:T(8,128)(2,1)S(1)} %copy-done.40, bf16[512,768]{1,0:T(8,128)(2,1)S(1)} %copy-done.38, bf16[512,768]{1,0:T(8,128)(2,1)S(1)} %copy-done.36, bf16[512,768]{1,0:T(8,128)(2,1)S(1)} %copy-done.6, f32[768]{0:T(1024)S(1)} %copy-done.51, f32[512]{0:T(512)S(1)} %copy-done.52), kind=kOutput, calls=%fused_computation | convolution fusion | flops 1822359552 | bytes 6689792 | tf_op jit(solution)/shard_map/dot_general | solution.py:835
  267.8 105.0 %scatter_all.1 = (bf16[2,256,768]{2,1,0:T(8,128)(2,1)}, bf16[2,256,768]{2,1,0:T(8,128)(2,1)}, f32[64,768]{1,0:T(8,128)}, f32[24,2048]{1,0:T(8,128)}, f32[24,2048...) custom-call(bf16[512,768]{1,0:T(8,128)(2,1)} %add_convert_fusion.out_ref, ...), custom_call_target="tpu_custom_call" | custom-call | tf_op jit(solution)/shard_map/scatter_all/pallas_call | solution.py:533
  374.1 2.1 copy.56
  (176 shorter events, 46.8 us)
Async XLA Ops:
  0.8 140.3 %copy-start.19 = (s32[2]{0:T(128)}, s32[2]{0:T(128)S(1)}, u32[]{:S(2)}) copy-start(s32[2]{0:T(128)S(1)} %get-tuple-element.120.blk_ref) | copy-start | bytes 28
  11.6 105.9 %copy-start.55 = (s32[2,1,4]{2,1,0:T(1,128)S(1)}, s32[2,1,4]{2,1,0:T(1,128)}, u32[]{:S(2)}) copy-start(s32[2,1,4]{2,1,0:T(1,128)} %param.23) | copy-start | bytes 100
  116.3 55.2 %copy-start.4 = (bf16[512,768]{1,0:T(8,128)(2,1)}, bf16[512,768]{1,0:T(8,128)(2,1)S(1)}, u32[]{:S(2)}) copy-start(bf16[512,768]{1,0:T(8,128)(2,1)S(1)} %get-tuple-element.90) | copy-start | bytes 2359300
  116.3 75.4 %copy-start.7 = (bf16[512,768]{1,0:T(8,128)(2,1)}, bf16[512,768]{1,0:T(8,128)(2,1)S(1)}, u32[]{:S(2)}) copy-start(bf16[512,768]{1,0:T(8,128)(2,1)S(1)} %get-tuple-element.99) | copy-start | bytes 2359300
  117.7 23.3 %copy-start.18 = (s32[512]{0:T(512)}, s32[512]{0:T(512)S(1)}, u32[]{:S(2)}) copy-start(s32[512]{0:T(512)S(1)} %get-tuple-element.117) | copy-start | bytes 6148
  120.4 20.7 %copy-start.2 = (s32[1024,1]{1,0:T(8,128)}, s32[1024,1]{1,0:T(8,128)S(1)}, u32[]{:S(2)}) copy-start(s32[1024,1]{1,0:T(8,128)S(1)} %copy.38.segk_ref) | copy-start | bytes 12292
  126.1 3.1 copy-start.51
  126.1 3.1 copy-start.52
  137.2 3.9 %copy-start.1 = (bf16[512,768]{1,0:T(8,128)(2,1)}, bf16[512,768]{1,0:T(8,128)(2,1)S(1)}, u32[]{:S(2)}) copy-start(bf16[512,768]{1,0:T(8,128)(2,1)S(1)} %get-tuple-element.125.q_ref) | copy-start | bytes 2359300
  141.1 30.4 %copy-start = (bf16[1024,1536]{1,0:T(8,128)(2,1)}, bf16[1024,1536]{1,0:T(8,128)(2,1)S(1)}, u32[]{:S(2)}) copy-start(bf16[1024,1536]{1,0:T(8,128)(2,1)S(1)} %share_kv.1.kv_ref) | copy-start | bytes 9437188
  182.6 7.0 %copy-start.56 = (bf16[512,2048]{1,0:T(8,128)(2,1)}, bf16[512,2048]{1,0:T(8,128)(2,1)S(1)}, u32[]{:S(2)}) copy-start(bf16[512,2048]{1,0:T(8,128)(2,1)S(1)} %get-tuple-element.121) | copy-start | bytes 6291460
  182.6 5.1 %copy-start.58 = (bf16[512,2048]{1,0:T(8,128)(2,1)S(1)}, bf16[512,2048]{1,0:T(8,128)(2,1)}, u32[]{:S(2)}) copy-start(bf16[512,2048]{1,0:T(8,128)(2,1)} %get-tuple-element.122) | copy-start | bytes 6291460
  238.3 5.4 %copy-start.9 = (bf16[512,768]{1,0:T(8,128)(2,1)S(1)}, bf16[512,768]{1,0:T(8,128)(2,1)}, u32[]{:S(2)}) copy-start(bf16[512,768]{1,0:T(8,128)(2,1)} %copy-done.8) | copy-start | bytes 2359300
  238.4 5.4 %copy-start.34 = (f32[512,768]{1,0:T(8,128)S(1)}, f32[512,768]{1,0:T(8,128)}, u32[]{:S(2)}) copy-start(f32[512,768]{1,0:T(8,128)} %copy-done.33) | copy-start | bytes 4718596
  247.4 11.1 %copy-start.39 = (bf16[512,768]{1,0:T(8,128)(2,1)}, bf16[512,768]{1,0:T(8,128)(2,1)S(1)}, u32[]{:S(2)}) copy-start(bf16[512,768]{1,0:T(8,128)(2,1)S(1)} %slice.259) | copy-start | bytes 2359300
  247.4 3.6 copy-start.59
  258.5 3.0 copy-start.35
  258.5 3.0 copy-start.37
  263.9 3.9 %copy-start.44 = (bf16[32,8,128]{2,1,0:T(8,128)(2,1)}, bf16[32,8,128]{2,1,0:T(8,128)(2,1)S(1)}, u32[]{:S(2)}) copy-start(bf16[32,8,128]{2,1,0:T(8,128)(2,1)S(1)} %scatter.24.refs_5_) | copy-start | bytes 196612
  372.8 3.4 copy-start.41
  374.1 3.0 copy-start.45
  374.1 3.7 copy-start.49
  374.1 4.3 %copy-start.48 = (f32[24,2048]{1,0:T(8,128)S(1)}, f32[24,2048]{1,0:T(8,128)}, u32[]{:S(2)}) copy-start(f32[24,2048]{1,0:T(8,128)} %get-tuple-element.178) | copy-start | bytes 589828
  376.2 3.6 copy-start.46
  (36 other events, 60.3 us)

commit v2 on v0

v2 whole, which is shorter than its diff:
```python
import functools

import jax
import jax.numpy as jnp
import numpy as np
from jax import lax
from jax.experimental import pallas as pl
from jax.experimental.pallas import tpu as pltpu
from jax.sharding import PartitionSpec as P

HEADS = 12
BLK = 256
SLOTS = 8
eps_norm = 1e-05
rope_base = 10000.0
MESH = pl.DeviceIdType.MESH
F32, BF16 = jnp.float32, jnp.bfloat16
NT = (((1,), (1,)), ((), ()))
TN = (((0,), (0,)), ((), ()))
ANY = pl.BlockSpec(memory_space=pl.ANY)
VM = pl.BlockSpec(memory_space=pltpu.VMEM)
SM = pl.BlockSpec(memory_space=pltpu.SMEM)


class Place:
    def __init__(self, ndp, nctx, pre=1):
        self.ndp, self.nctx, self.pre = ndp, nctx, pre
        self.nz = nctx // pre
        self.nb = 2
        self.na = ndp // 4
        self.g = nctx // 2
        self.gz = nctx // 4
        self.dp = lax.axis_index("dp")
        self.ctx = lax.axis_index("ctx")
        self.k, self.core = self.dp // 2, self.dp % 2
        self.ya, self.xb = self.k // self.nb, self.k % self.nb
        self.me = self.dp * nctx + self.ctx
        self.zi = self.ctx // pre
        self.pack = self.ctx // self.gz
        self.j = self.core * self.gz + self.ctx % self.gz

    def member(self, j):
        return (self.k * 2 + j // self.gz, self.pack * self.gz + j % self.gz)

    def holder(self, m, d, c):
        j = jnp.where(c < self.g, c, 2 * self.g - 1 - c)
        return ((d // 2) * 2 + j // self.gz, (m * 2 + d % 2) * self.gz + j % self.gz)

    def dp_of(self, ya, xb, core):
        return (ya * self.nb + xb) * 2 + core


def greet_all(pc):
    total = pc.ndp * pc.nctx
    barrier = pltpu.get_barrier_semaphore()

    def greet(i, carry):
        other = (pc.me + i) % total
        pl.semaphore_signal(
            barrier, inc=1, device_id=(other // pc.nctx, other % pc.nctx), device_id_type=MESH
        )
        return carry

    lax.fori_loop(1, total, greet, 0)


def met_all(pc):
    pl.semaphore_wait(pltpu.get_barrier_semaphore(), pc.ndp * pc.nctx - 1)


def remote(src, dst, ss, rs, dev):
    return pltpu.make_async_remote_copy(
        src_ref=src, dst_ref=dst, send_sem=ss, recv_sem=rs, device_id=dev, device_id_type=MESH
    )


class Gather:
    def __init__(self, pc, shards, full, chunks, sems):
        self.pc, self.shards, self.full, self.chunks = pc, shards, full, chunks
        (
            self.own_sem, self.z_ss, self.z_rs, self.x_ss, self.x_rs, self.y_ss, self.y_rs,
            self.fa_ss, self.fa_rs, self.fb_ss, self.fb_rs, self.c_ss, self.c_rs,
        ) = sems

    def cut(self, ref, t, start, count):
        _, c0, cw = self.chunks[t]
        return ref.at[pl.ds(pl.multiple_of(start, 8), count), pl.ds(c0, cw)]

    def rows(self, t):
        return self.shards[self.chunks[t][0]].shape[0]

    def mine(self, t):
        a, c0, cw = self.chunks[t]
        return self.shards[a].at[:, pl.ds(c0, cw)]

    def place(self, t, zi=None, count=1):
        r = self.rows(t)
        zi = self.pc.zi if zi is None else zi
        return self.cut(self.full[self.chunks[t][0]], t, (self.pc.dp * self.pc.nz + zi) * r, count * r)

    def block(self, t, dp, part=None):
        n = self.pc.nz * self.rows(t)
        ref = self.full[self.chunks[t][0]]
        if part is None:
            return self.cut(ref, t, dp * n, n)
        return self.cut(ref, t, dp * n + part * (n // 2), n // 2)

    def own_copy(self, t):
        return pltpu.make_async_copy(self.mine(t), self.place(t), self.own_sem.at[t])

    def z_copies(self, t):
        pc = self.pc
        return [
            remote(
                self.mine(t), self.place(t), self.z_ss.at[t, d - 1], self.z_rs.at[t, d - 1],
                (pc.dp, (pc.ctx + d * pc.pre) % pc.nctx),
            )
            for d in range(1, pc.nz)
        ]


    def paired(self, t):
        return self.pc.nz == 4 and t >= STRAIGHT

    def pair_copies(self, t):
        pc = self.pc
        pair = pc.zi + 1 - 2 * (pc.zi % 2)
        near, far = pc.zi // 2 * 2, 2 - pc.zi // 2 * 2

        def at(z):
            return (pc.dp, pc.ctx + (z - pc.zi) * pc.pre)

        def copy(src, dst, i, z):
            return remote(src, dst, self.z_ss.at[t, i], self.z_rs.at[t, i], at(z))

        return (
            copy(self.mine(t), self.place(t), 0, pair),
            copy(self.place(t, near, 2), self.place(t, near, 2), 1, 3 - pc.zi),
            copy(self.place(t, far, 2), self.place(t, far, 2), 2, pair),
        )

    def inner(self):
        return (self.pc.zi == 1) | (self.pc.zi == 2)

    def z_start(self, t):
        if self.paired(t):
            self.pair_copies(t)[0].start()
        else:
            start_all(self.z_copies(t))

    def z_middle(self, t):
        self.own_copy(t).wait()
        if self.paired(t):
            own, both, _on = self.pair_copies(t)

            @pl.when(self.inner())
            def _():
                own.wait_recv()
                both.start()

    def z_finish(self, t):
        if self.paired(t):
            own, both, on = self.pair_copies(t)

            @pl.when(self.inner())
            def _():
                both.wait_recv()
                on.start()

            @pl.when(jnp.logical_not(self.inner()))
            def _():
                own.wait_recv()
                on.wait_recv()

        else:
            wait_arrived(self.z_copies(t))

    def z_sent(self, t):
        if self.paired(t):
            own, both, on = self.pair_copies(t)
            own.wait_send()

            @pl.when(self.inner())
            def _():
                both.wait_send()
                on.wait_send()

        else:
            for cp in self.z_copies(t):
                cp.wait_send()

    def xy_copies(self, t):
        pc = self.pc
        out = []
        for d in range(1, pc.nb):
            to = (pc.dp_of(pc.ya, (pc.xb + d) % pc.nb, pc.core), pc.ctx)
            out.append(
                remote(
                    self.block(t, pc.dp), self.block(t, pc.dp),
                    self.x_ss.at[t, d - 1], self.x_rs.at[t, d - 1], to,
                )
            )
        for d in range(1, pc.na):
            to = (pc.dp_of((pc.ya + d) % pc.na, pc.xb, pc.core), pc.ctx)
            out.append(
                remote(
                    self.block(t, pc.dp), self.block(t, pc.dp),
                    self.y_ss.at[t, d - 1], self.y_rs.at[t, d - 1], to,
                )
            )
        return out

    def forward_copies(self, t):
        pc = self.pc
        out = []
        for dx in range(1, pc.nb):
            for dy in range(1, pc.na):
                src = pc.dp_of(pc.ya, (pc.xb + pc.nb - dx) % pc.nb, pc.core)
                out.append(
                    remote(
                        self.block(t, src, 0), self.block(t, src, 0),
                        self.fa_ss.at[t, dx - 1, dy - 1], self.fa_rs.at[t, dx - 1, dy - 1],
                        (pc.dp_of((pc.ya + dy) % pc.na, pc.xb, pc.core), pc.ctx),
                    )
                )
                src = pc.dp_of((pc.ya + pc.na - dy) % pc.na, pc.xb, pc.core)
                out.append(
                    remote(
                        self.block(t, src, 1), self.block(t, src, 1),
                        self.fb_ss.at[t, dx - 1, dy - 1], self.fb_rs.at[t, dx - 1, dy - 1],
                        (pc.dp_of(pc.ya, (pc.xb + dx) % pc.nb, pc.core), pc.ctx),
                    )
                )
        return out

    def core_copy(self, t, dy, dx):
        pc = self.pc
        src = pc.dp_of((pc.ya + pc.na - dy) % pc.na, (pc.xb + pc.nb - dx) % pc.nb, pc.core)
        return remote(
            self.block(t, src), self.block(t, src), self.c_ss.at[t, dy, dx], self.c_rs.at[t, dy, dx],
            (pc.k * 2 + 1 - pc.core, pc.ctx),
        )

    def core_copies(self, t, which):
        pc = self.pc
        pairs = {
            "own": [(0, 0)],
            "xy": [(0, dx) for dx in range(1, pc.nb)] + [(dy, 0) for dy in range(1, pc.na)],
            "diag": [(dy, dx) for dy in range(1, pc.na) for dx in range(1, pc.nb)],
        }[which]
        return [self.core_copy(t, dy, dx) for dy, dx in pairs]

    def step(self, t, stage):
        if stage == 0:
            self.z_start(t)
        elif stage == -1:
            self.z_middle(t)
        elif stage == 1:
            self.z_finish(t)
            start_all(self.xy_copies(t) + self.core_copies(t, "own"))
        elif stage == 2:
            wait_arrived(self.xy_copies(t))
            start_all(self.forward_copies(t) + self.core_copies(t, "xy"))
        elif stage == 3:
            wait_arrived(self.forward_copies(t))
            start_all(self.core_copies(t, "diag"))
        else:
            wait_arrived([cp for w in ("own", "xy", "diag") for cp in self.core_copies(t, w)])

    def wait_sent(self):
        for t in range(len(self.chunks)):
            self.z_sent(t)
            for cp in self.xy_copies(t) + self.forward_copies(t):
                cp.wait_send()
            for w in ("own", "xy", "diag"):
                for cp in self.core_copies(t, w):
                    cp.wait_send()


def start_all(copies):
    for cp in copies:
        cp.start()


def wait_arrived(copies):
    for cp in copies:
        cp.wait_recv()


class Steps:
    def __init__(self):
        self.todo = []
        self.done = set()

    def add(self, name, fn):
        self.todo.append((name, fn))

    def run(self, count=1):
        for _ in range(count):
            if self.todo:
                name, fn = self.todo.pop(0)
                fn()
                self.done.add(name)

    def until(self, name):
        while name not in self.done:
            self.run()

    def take(self, count):
        out, self.todo = self.todo[:count], self.todo[count:]
        for name, _ in out:
            self.done.add(name)
        return [fn for _, fn in out]


def loop_with_steps(n, body, groups):
    def one(i, carry):
        body(i)
        for at, group in enumerate(groups):
            if group:

                @pl.when(i == at)
                def _():
                    for fn in group:
                        fn()

        return carry

    lax.fori_loop(0, n, one, 0)


def lane_swap(u):
    lane = lax.broadcasted_iota(jnp.int32, (1, 128), 1) % 64
    return jnp.where(lane < 32, pltpu.roll(u, 96, 1), pltpu.roll(u, 32, 1))


def turned(u, cos_t, sin_t):
    parts = []
    for i in range(u.shape[1] // 128):
        v = u[:, i * 128 : (i + 1) * 128]
        parts.append(v * cos_t + lane_swap(v) * sin_t)
    return jnp.concatenate(parts, axis=1)


def cols(i, size=256):
    return pl.ds(pl.multiple_of(i * size, size), size)


def layer_rows(pc, half):
    return pc.j if half == 0 else 2 * pc.g - 1 - pc.j


def gain_row(tiles, which, share, width):
    lane = lax.broadcasted_iota(jnp.int32, (128, width), 0)
    col = lax.broadcasted_iota(jnp.int32, (128, width), 1)
    spread = (lane == col % share).astype(BF16)
    wide = jnp.dot(tiles, spread, preferred_element_type=F32)
    row = lax.broadcasted_iota(jnp.int32, wide.shape, 0)
    col = lax.broadcasted_iota(jnp.int32, wide.shape, 1)
    keep = row == SLOTS * (col // share) + which
    return jnp.sum(jnp.where(keep, wide, 0.0), axis=0, keepdims=True)


class Scatter:
    def __init__(self, pc, grads, shares, bufs, sems):
        self.pc, self.grads, self.shares = pc, grads, shares
        self.core_in, self.diag_a, self.diag_b, self.x_in, self.y_in, self.z_in = bufs
        (
            self.c_ss, self.c_rs, self.da_ss, self.da_rs, self.db_ss, self.db_rs,
            self.x_ss, self.x_rs, self.y_ss, self.y_rs, self.z_ss, self.z_rs,
        ) = sems
        self.yx = [(dy, dx) for dy in range(1, pc.na) for dx in range(1, pc.nb)]
        self.yx += [(0, dx) for dx in range(1, pc.nb)] + [(dy, 0) for dy in range(1, pc.na)]
        self.yx += [(0, 0)]

    def first(self, dy, dx, core):
        pc = self.pc
        k = ((pc.ya + dy) % pc.na) * pc.nb + (pc.xb + dx) % pc.nb
        return (k * 2 + core) * pc.nz

    def core_copies(self, t):
        pc = self.pc
        return [
            remote(
                self.grads[t].at[pl.ds(self.first(dy, dx, 1 - pc.core), pc.nz)],
                self.core_in[t].at[dy, dx], self.c_ss.at[t, dy, dx], self.c_rs.at[t, dy, dx],
                (pc.k * 2 + 1 - pc.core, pc.ctx),
            )
            for dy, dx in self.yx
        ]

    def diag_copies(self, t):
        pc = self.pc
        h = pc.nz // 2
        out = []
        for dy in range(1, pc.na):
            for dx in range(1, pc.nb):
                out.append(
                    remote(
                        self.core_in[t].at[dy, dx, pl.ds(0, h)], self.diag_a[t].at[dy - 1, dx - 1],
                        self.da_ss.at[t, dy - 1, dx - 1], self.da_rs.at[t, dy - 1, dx - 1],
                        (pc.dp_of((pc.ya + dy) % pc.na, pc.xb, pc.core), pc.ctx),
                    )
                )
                out.append(
                    remote(
                        self.core_in[t].at[dy, dx, pl.ds(h, h)], self.diag_b[t].at[dy - 1, dx - 1],
                        self.db_ss.at[t, dy - 1, dx - 1], self.db_rs.at[t, dy - 1, dx - 1],
                        (pc.dp_of(pc.ya, (pc.xb + dx) % pc.nb, pc.core), pc.ctx),
                    )
                )
        return out

    def xy_copies(self, t):
        pc = self.pc
        out = []
        for dx in range(1, pc.nb):
            out.append(
                remote(
                    self.core_in[t].at[0, dx], self.x_in[t].at[dx - 1],
                    self.x_ss.at[t, dx - 1], self.x_rs.at[t, dx - 1],
                    (pc.dp_of(pc.ya, (pc.xb + dx) % pc.nb, pc.core), pc.ctx),
                )
            )
        for dy in range(1, pc.na):
            out.append(
                remote(
                    self.core_in[t].at[dy, 0], self.y_in[t].at[dy - 1],
                    self.y_ss.at[t, dy - 1], self.y_rs.at[t, dy - 1],
                    (pc.dp_of((pc.ya + dy) % pc.na, pc.xb, pc.core), pc.ctx),
                )
            )
        return out

    def z_copies(self, t):
        pc = self.pc
        return [
            remote(
                self.core_in[t].at[0, 0, (pc.zi + d) % pc.nz], self.z_in[t].at[d - 1],
                self.z_ss.at[t, d - 1], self.z_rs.at[t, d - 1],
                (pc.dp, (pc.ctx + d * pc.pre) % pc.nctx),
            )
            for d in range(1, pc.nz)
        ]

    def step(self, t, stage):
        pc = self.pc
        h = pc.nz // 2
        if stage == 0:
            start_all(self.core_copies(t))
        elif stage == 1:
            wait_arrived(self.core_copies(t))
            for dy, dx in self.yx:
                first = self.first(dy, dx, pc.core)
                self.accumulate(t, dy, dx, 0, pc.nz, [lambda z, f=first: self.grads[t][f + z]])
            start_all(self.diag_copies(t))
        elif stage == 2:
            for cp in self.core_copies(t):
                cp.wait_send()
            wait_arrived(self.diag_copies(t))
            for dx in range(1, pc.nb):
                self.accumulate(
                    t, 0, dx, 0, h,
                    [lambda z, dy=dy: self.diag_a[t][dy - 1, dx - 1, z] for dy in range(1, pc.na)],
                )
            for dy in range(1, pc.na):
                self.accumulate(
                    t, dy, 0, h, h,
                    [lambda z, dx=dx: self.diag_b[t][dy - 1, dx - 1, z] for dx in range(1, pc.nb)],
                )
            start_all(self.xy_copies(t))
        elif stage == 3:
            wait_arrived(self.xy_copies(t))
            self.accumulate(
                t, 0, 0, 0, pc.nz,
                [lambda z, i=i: self.x_in[t][i, z] for i in range(pc.nb - 1)]
                + [lambda z, i=i: self.y_in[t][i, z] for i in range(pc.na - 1)],
            )
            start_all(self.z_copies(t))
        else:
            wait_arrived(self.z_copies(t))
            total = self.core_in[t][0, 0, pc.zi].astype(F32)
            for i in range(pc.nz - 1):
                total = total + self.z_in[t][i].astype(F32)
            self.shares[t][...] = total

    def accumulate(self, t, dy, dx, z0, count, others):
        ref = self.core_in[t]

        def one(z, carry):
            total = ref[dy, dx, z0 + z].astype(F32)
            for other in others:
                total = total + other(z).astype(F32)
            ref[dy, dx, z0 + z] = total.astype(BF16)
            return carry

        lax.fori_loop(0, count, one, 0)

    def wait_sent(self):
        for t in range(len(self.grads)):
            for cp in self.diag_copies(t) + self.xy_copies(t) + self.z_copies(t):
                cp.wait_send()


class Rounds(Steps):
    def __init__(self, scatter, stages):
        super().__init__()
        self.scatter, self.stages = scatter, stages
        self.last = []

    def begin(self, t):
        self.scatter.step(t, 0)
        self.todo.append((t, 1))

    def take(self, count):
        out = []
        for _ in range(count):
            if self.todo:
                t, stage = self.todo.pop(0)
                out.append(functools.partial(self.scatter.step, t, stage))
                if stage + 1 < self.stages - 1:
                    self.todo.append((t, stage + 1))
                else:
                    self.last.append(t)
        return out

    def finish(self):
        while self.todo:
            self.run()
        for t in self.last:
            self.scatter.step(t, self.stages - 1)

    def run(self, count=1):
        for fn in self.take(count):
            fn()

    def push(self, *chunks):
        for t in chunks:
            i = [c for c, _ in self.todo].index(t)
            self.todo.insert(0, self.todo.pop(i))
            self.run(1)


def block_at(ref, index, size=BLK):
    return ref.at[pl.ds(pl.multiple_of(index * size, size), size)]


NEG = -1e30


def lane_mask(h):
    lanes = lax.broadcasted_iota(jnp.int32, (1, 128), 1)
    return (lanes < 64) if h == 0 else (lanes >= 64)


def inverse_rms(values):
    return lax.rsqrt(jnp.mean(values * values, axis=-1, keepdims=True) + eps_norm)


def norm_back(grad, values, inverse, gain):
    scaled = grad * gain
    mean = jnp.mean(scaled * values, axis=-1, keepdims=True)
    return (
        inverse * scaled - values * (inverse * inverse * inverse) * mean,
        jnp.sum(grad * values * inverse, axis=0),
    )


AHEAD = 5
BEFORE_X = ('xy', 4)
STRAIGHT = 4
LOOP_ROUNDS = (2, 2, 2, 1, 1, 1)
ORDER_BEFORE = ()
ORDER_AT = {0: (0,), 1: (1,), 2: (2,), 3: (3,), 4: (4,), 5: (5,), 6: (6,), 7: (7,)}
CHUNKS = ("gate0", "up0", "gate1", "up1", "down0", "down1", "down2", "out", "q", "k", "v", "gain")


def layer_kernel(
    ndp, nctx, pre, share, chunks, order_ref, len_ref, freq_ref, x_hbm, dy_hbm, *refs
):
    nt, nch = 6, len(CHUNKS)
    shards, refs = refs[:nt], refs[nt:]
    full, refs = refs[:nt], refs[nt:]
    fin, refs = refs[:2], refs[2:]
    (s_qkv, s_out, s_gate, s_up, s_down, s_gain), refs = refs[:6], refs[6:]
    (b_gate0, b_up0, b_gate1, b_up1, b_down, b_out, b_gain), refs = refs[:7], refs[7:]
    bufs = [refs[i * nch : (i + 1) * nch] for i in range(6)]
    refs = refs[6 * nch :]
    (
        x_v, dy_v, kv_v, dkv_in, tok, plen, hid_v, q_v, lse_v, att_t, n1_t, rope_v, bias_v, gb_v, out_v,
        gain_v, dg_v, tiles_v,
        tok_ss, tok_rs, ret_ss, ret_rs, len_ss, len_rs, kv_ss, kv_rs, dkv_ss, dkv_rs, load_sem, fin_sem,
        *sems,
    ) = refs
    pc = Place(ndp, nctx, pre)
    rows, width = x_v.shape
    ff = s_gate.shape[1]
    half_ff, third = ff // 2, width // 3
    slot = BLK // ndp
    n_blocks = ndp * pc.nz
    gather = Gather(pc, shards, full, chunks, sems[:13])
    narrow = slice(0, width)
    grads = [b_gate0, b_up0, b_gate1, b_up1]
    grads += [b_down.at[:, :, i * third : (i + 1) * third] for i in range(3)] + [b_out]
    grads += [b.at[:, :, narrow] for b in (b_gate0, b_up0, b_gate1)] + [b_gain]
    shares = [s_gate.at[:, pl.ds(0, half_ff)], s_up.at[:, pl.ds(0, half_ff)]]
    shares += [s_gate.at[:, pl.ds(half_ff, half_ff)], s_up.at[:, pl.ds(half_ff, half_ff)]]
    shares += [s_down.at[:, pl.ds(i * third, third)] for i in range(3)] + [s_out]
    shares += [s_qkv.at[:, pl.ds(i * width, width)] for i in range(3)] + [s_gain]
    scatter = Scatter(pc, grads, shares, bufs, sems[13:])
    rounds = Rounds(scatter, 5)
    chunk = {name: i for i, name in enumerate(CHUNKS)}
    partner = (pc.k * 2 + 1 - pc.core, pc.ctx)
    last_of = {a: max(t for t in range(len(chunks)) if chunks[t][0] == a) for a in range(nt)}
    loads = {}

    def load(name, src, dst):
        loads[name] = (src, dst, len(loads))
        pltpu.make_async_copy(src, dst, load_sem.at[loads[name][2]]).start()

    def ready(*names):
        for name in names:
            src, dst, i = loads[name]
            pltpu.make_async_copy(src, dst, load_sem.at[i]).wait()


    def to_pack(perm, t, m, d):
        dp_to, ctx_to = pc.holder(m, d, pc.ctx)
        half = jnp.where(pc.ctx < pc.g, 0, 1)
        src = perm.at[t, m, pl.ds(pl.multiple_of(d * slot, slot), slot)]
        dst = (x_v, dy_v)[t].at[pl.ds(pl.multiple_of(half * BLK + pc.dp * slot, slot), slot)]
        rs = tok_rs.at[t, half, pc.dp]
        same = (dp_to == pc.dp) & (ctx_to == pc.ctx)
        return same, src, dst, tok_ss.at[t, m, d], rs, (dp_to, ctx_to)

    def to_loader(t, half, b):
        c = layer_rows(pc, half)
        d = pc.k * 2 + pc.pack % 2
        m = pc.pack // 2
        src = (out_v, gb_v)[t].at[pl.ds(pl.multiple_of(half * BLK + b * slot, slot), slot)]
        dst = tok.at[t, m, pl.ds(pl.multiple_of(d * slot, slot), slot)]
        same = (b == pc.dp) & (c == pc.ctx)
        return same, src, dst, ret_ss.at[t, half, b], ret_rs.at[t, m, d], (b, c)

    def send_group(find, gy, gx):
        k = ((pc.ya + gy) % pc.na) * pc.nb + (pc.xb + gx) % pc.nb
        for first in range(2):
            for e in range(2):
                same, src, dst, ss, rs, to = find(first, 2 * k + e)

                @pl.when(same)
                def _():
                    pltpu.make_async_copy(src, dst, rs).start()

                @pl.when(jnp.logical_not(same))
                def _():
                    remote(src, dst, ss, rs, to).start()

    def tokens_sent(find):
        def one(d, carry):
            same, src, dst, ss, rs, to = find(d)

            @pl.when(jnp.logical_not(same))
            def _():
                remote(src, dst, ss, rs, to).wait_send()

            return carry

        lax.fori_loop(0, ndp, one, 0)

    def tokens_arrived(ref, sem_of, base):
        def one(b, carry):
            dst = ref.at[pl.ds(pl.multiple_of(base + b * slot, slot), slot)]
            pltpu.make_async_copy(dst, dst, sem_of(b)).wait()
            return carry

        lax.fori_loop(0, ndp, one, 0)

    def send_back(t):
        for gy, gx in offsets:
            send_group(functools.partial(to_loader, t), gy, gx)

    offsets = [(gy, gx) for gy in range(pc.na) for gx in range(pc.nb)]

    def fin_copy(t):
        return pltpu.make_async_copy(tok.at[t], fin[t], fin_sem.at[t])

    def place_tokens(t):
        for half in range(2):
            tokens_sent(functools.partial(to_loader, t, half))
        for m in range(2):
            tokens_arrived(tok.at[t, m], lambda d, m=m: ret_rs.at[t, m, d], 0)
            hot = (lax.broadcasted_iota(jnp.int32, (BLK, BLK), 0) == order_ref[m]).astype(BF16)
            tok[t, m] = jnp.dot(hot, tok[t, m], preferred_element_type=F32).astype(BF16)
        fin_copy(t).start()

    steps = Steps()
    len_copy = functools.partial(remote, len_ref, plen, len_ss, len_rs, partner)

    def plan(perm):
        n = len(chunks)
        groups = [(t, gy, gx) for t in range(2) for gy, gx in offsets]

        def tokens(i):
            t, gy, gx = groups[i]
            steps.add(("tok", i), functools.partial(send_group, functools.partial(to_pack, perm, t), gy, gx))

        each = len(offsets) // 4

        def some_tokens(q):
            for i in range(q * each, (q + 1) * each):
                tokens(i)

        def middle(i):
            steps.add(("mid", i), functools.partial(gather.step, i, -1))

        for i in range(2):
            middle(i)
        for i in ORDER_BEFORE:
            some_tokens(i)
        for i in range(n + 3):
            if i >= 3:
                steps.add(("c", i - 3), functools.partial(gather.step, i - 3, 4))
            if i < n:
                steps.add(("z", i), functools.partial(gather.step, i, 1))
                if i + 2 < n:
                    middle(i + 2)
                if i + AHEAD < n:
                    steps.add(("start", i + AHEAD), functools.partial(gather.step, i + AHEAD, 0))
                for q in ORDER_AT.get(i, ()):
                    some_tokens(q)
            if 1 <= i <= n:
                steps.add(("xy", i - 1), functools.partial(gather.step, i - 1, 2))
            if 2 <= i <= n + 1:
                steps.add(("f", i - 2), functools.partial(gather.step, i - 2, 3))
        return len(groups)

    def index(shape, axis):
        return lax.broadcasted_iota(jnp.int32, shape, axis).astype(F32)

    def attention_forward(perm, wqkv, wout, n1_v, att_v):
        load("x_in", x_hbm, perm.at[0])
        load("dy_in", dy_hbm, perm.at[1])
        for t in range(len(chunks)):
            gather.own_copy(t).start()
        greet_all(pc)
        for t, name in enumerate(("x_in", "dy_in")):
            ready(name)
            for m in range(2):
                hot = (lax.broadcasted_iota(jnp.int32, (BLK, BLK), 0) == order_ref[m]).astype(BF16)
                perm[t, m] = lax.dot_general(
                    hot, perm[t, m], TN, preferred_element_type=F32
                ).astype(BF16)
        met_all(pc)
        for t in range(AHEAD):
            gather.step(t, 0)
        len_copy().start()
        n_groups = plan(perm)
        steps.until(("xy", 0))

        len_copy().wait_recv()
        lens = jnp.where(pc.pack % 2 == pc.core, len_ref[...], plen[...]).astype(F32)
        lens = jnp.where(pc.pack // 2 == 0, lens[0:1], lens[1:2])
        lane = lax.broadcasted_iota(jnp.int32, (1, 128), 1)
        ends = [jnp.sum(jnp.where(lane <= i, lens, 0.0), axis=1, keepdims=True) for i in range(4)]
        sizes = [jnp.sum(jnp.where(lane == i, lens, 0.0), axis=1, keepdims=True) for i in range(4)]

        def segment(at):
            seg = jnp.zeros(at.shape, F32)
            start = jnp.zeros(at.shape, F32)
            for end, size in zip(ends, sizes):
                passed = (at >= end).astype(F32)
                seg = seg + passed
                start = start + passed * size
            return seg, start

        sign = jnp.where(lane % 64 < 32, -1.0, 1.0)
        at = 0
        for half in range(2):
            base = (layer_rows(pc, half) * BLK).astype(F32)
            here = base + index((BLK, 128), 0)
            _, start = segment(here)
            angle = (here - start) * freq_ref[0:1]
            rope_v[half * BLK : (half + 1) * BLK, 0:128] = jnp.cos(angle)
            rope_v[half * BLK : (half + 1) * BLK, 128:256] = jnp.sin(angle) * sign
            qrow = base + index((1, BLK), 1)
            segq, _ = segment(qrow)
            for kb in range((half + 1) * pc.g):
                krow = kb * BLK + index((BLK, BLK), 0)
                segk, _ = segment(kb * BLK + index((BLK, 1), 0))
                bias_v[at : at + BLK] = jnp.where((segk == segq) & (krow <= qrow), 0.0, NEG).astype(BF16)
                at += BLK
        steps.until(("c", 0))
        load("tiles", full[0], tiles_v)
        ready("tiles")
        gain_v[0:1] = gain_row(tiles_v[...], 0, share, width)
        gain_v[1:2] = gain_row(tiles_v[...], 1, share, width)
        steps.until(("tok", n_groups // 2 - 1))
        steps.until(BEFORE_X)
        for half in range(2):
            tokens_arrived(x_v, lambda b, half=half: tok_rs.at[0, half, b], half * BLK)
        x = x_v[...].astype(F32)
        n1_v[...] = (x * inverse_rms(x) * gain_v[0:1]).astype(BF16)
        n1_t[...] = n1_v[...].T
        steps.run(2)

        cos_t, sin_t = rope_v[:, 0:128], rope_v[:, 128:256]

        def kv_copies(part):
            copies = []
            for half in range(2):
                ref = kv_v.at[
                    pl.ds(pl.multiple_of(layer_rows(pc, half) * BLK, BLK), BLK),
                    pl.ds(part * width, width),
                ]
                for o in range(1, pc.g):
                    copies.append(
                        remote(
                            ref, ref, kv_ss.at[part, half, o - 1], kv_rs.at[part, half, o - 1],
                            pc.member((pc.j + o) % pc.g),
                        )
                    )
            return copies

        def project(base, put, rope):
            def one(i, carry):
                u = jnp.dot(
                    n1_v[...], wqkv[:, pl.ds(pl.multiple_of(base + i * BLK, BLK), BLK)],
                    preferred_element_type=F32,
                )
                if rope:
                    u = turned(u, cos_t, sin_t)
                put(i, u.astype(BF16))
                return carry

            lax.fori_loop(0, width // BLK, one, 0)

        def to_kv(part):
            def put(i, u):
                for half in range(2):
                    kv_v[
                        pl.ds(pl.multiple_of(layer_rows(pc, half) * BLK, BLK), BLK),
                        pl.ds(pl.multiple_of(part * width + i * BLK, BLK), BLK),
                    ] = u[half * BLK : (half + 1) * BLK]

            return put

        def to_q(i, u):
            q_v[:, cols(i)] = u

        steps.until(("c", last_of[1]))
        load("wqkv", full[1], wqkv)
        ready("wqkv")
        project(width, to_kv(0), True)
        start_all(kv_copies(0))
        steps.run(1)
        project(2 * width, to_kv(1), False)
        start_all(kv_copies(1))
        steps.run(1)
        project(0, to_q, True)
        steps.run(2)
        wait_arrived(kv_copies(0) + kv_copies(1))

        def pair(hp):
            hc = cols(hp, 128)
            vc = pl.ds(pl.multiple_of(width + hp * 128, 128), 128)
            at = 0
            for half in range(2):
                nk = (half + 1) * pc.g * BLK
                rr = slice(half * BLK, (half + 1) * BLK)
                qp = q_v[rr, hc]
                both = []
                for h in range(2):
                    qm = (jnp.where(lane_mask(h), qp, 0) * 0.125).astype(BF16)
                    s = lax.dot_general(kv_v[0:nk, hc], qm, NT, preferred_element_type=F32)
                    s = s + bias_v[at : at + nk].astype(F32)
                    top = jnp.max(s, axis=0, keepdims=True)
                    p = jnp.exp(s - top)
                    total = jnp.sum(p, axis=0, keepdims=True)
                    p = (p * (1.0 / total)).astype(BF16)
                    both.append(
                        lax.dot_general(kv_v[0:nk, vc], p, TN, preferred_element_type=F32)
                    )
                    lse_v[hp, h : h + 1, rr] = top + jnp.log(total)
                sub = lax.broadcasted_iota(jnp.int32, (128, BLK), 0)
                o = jnp.where(sub < 64, both[0], both[1])
                att_v[rr, hc] = o.T.astype(BF16)
                att_t[hc, rr] = o.astype(BF16)
                at += nk

        loop_with_steps(HEADS // 2, pair, [steps.take(2) for _ in range(HEADS // 2)])
        steps.until(("c", last_of[2]))
        load("wout", full[2], wout)
        ready("wout")
        hid_v[...] = x_v[...].astype(F32) + jnp.dot(
            att_v[...], wout[...], preferred_element_type=F32
        )
        steps.until(("tok", n_groups - 1))
        for t in range(2):
            for m in range(2):
                tokens_sent(functools.partial(to_pack, perm, t, m))
        for half in range(2):
            tokens_arrived(dy_v, lambda b, half=half: tok_rs.at[1, half, b], half * BLK)
        for cp in kv_copies(0) + kv_copies(1):
            cp.wait_send()

    pl.run_scoped(
        attention_forward,
        pltpu.VMEM((2, 2, BLK, width), BF16), pltpu.VMEM((width, 3 * width), BF16),
        pltpu.VMEM((width, width), BF16), pltpu.VMEM((rows, width), BF16),
        pltpu.VMEM((rows, width), BF16),
    )


    def feed_forward(wdown, wgate, wup, n2_v, n2_t, gn2, res):
        hid = hid_v[...]
        n2_v[...] = (hid * inverse_rms(hid) * gain_v[1:2]).astype(BF16)
        n2_t[...] = n2_v[...].T
        res[...] = hid
        gn2[...] = jnp.zeros_like(gn2)
        steps.run(2)
        steps.until(("c", last_of[5]))
        load("wdown", full[5], wdown)
        n_half = half_ff // BLK
        per = BLK // b_down.shape[1]

        def part(which, c):
            cc = cols(c)
            rr = cols(which * n_half + c)
            g = jnp.dot(n2_v[...], wgate[:, cc], preferred_element_type=F32)
            u = jnp.dot(n2_v[...], wup[:, cc], preferred_element_type=F32)
            gi = lax.dot_general(dy_v[...], wdown[rr, :], NT, preferred_element_type=F32)
            sig = 1.0 / (1.0 + jnp.exp(-g))
            act = g * sig
            inner = (act * u).astype(BF16)
            gg = (gi * u * (sig * (1.0 + g * (1.0 - sig)))).astype(BF16)
            gu = (gi * act).astype(BF16)
            res[...] += jnp.dot(inner, wdown[rr, :], preferred_element_type=F32)
            gn2[...] += lax.dot_general(
                gg, wgate[:, cc], NT, preferred_element_type=F32
            ) + lax.dot_general(gu, wup[:, cc], NT, preferred_element_type=F32)
            for buf, value in (((b_gate0, b_gate1)[which], gg), ((b_up0, b_up1)[which], gu)):
                d = jnp.dot(n2_t[...], value, preferred_element_type=F32)
                buf[:, :, cc] = d.reshape(n_blocks, -1, BLK).astype(BF16)
            d = jnp.dot(inner.T, dy_v[...], preferred_element_type=F32)
            b_down[pl.ds((which * n_half + c) * per, per)] = d.reshape(per, -1, width).astype(BF16)

        def load_half(which):
            n = len(chunks)
            steps.until(("c", n - 3 if which == 0 else n - 1))
            cc = pl.ds(which * half_ff, half_ff)
            load(f"wgate{which}", full[3].at[:, cc], wgate)
            load(f"wup{which}", full[4].at[:, cc], wup)
            ready(f"wgate{which}", f"wup{which}")

        load_half(0)
        ready("wdown")
        loop_with_steps(n_half, functools.partial(part, 0), [steps.take(2) for _ in range(n_half)])
        rounds.begin(chunk["gate0"])
        rounds.begin(chunk["up0"])
        load_half(1)
        while steps.todo:
            steps.run()
        loop_with_steps(n_half, functools.partial(part, 1), [rounds.take(2) if i < 2 else [] for i in range(n_half)])
        for name in ("gate1", "up1", "down0", "down1", "down2"):
            rounds.begin(chunk[name])
        out_v[...] = res[...].astype(BF16)
        hid = hid_v[...]
        back, d_gain = norm_back(gn2[...], hid, inverse_rms(hid), gain_v[1:2])
        dg_v[1:2] = d_gain.reshape(1, width)
        gh = dy_v[...].astype(F32) + back
        hid_v[...] = gh
        gb_v[...] = gh.astype(BF16)
        rounds.push(*[chunk[name] for name in ("gate1", "up1", "down0", "down1", "down2")])

    pl.run_scoped(
        feed_forward,
        pltpu.VMEM((ff, width), BF16), pltpu.VMEM((width, half_ff), BF16),
        pltpu.VMEM((width, half_ff), BF16), pltpu.VMEM((rows, width), BF16),
        pltpu.VMEM((width, rows), BF16), pltpu.VMEM((rows, width), F32), pltpu.VMEM((rows, width), F32),
    )


    def head_pairs(gqkv, wout, gatt_v, acc):
        load("wout_back", full[2], wout)
        ready("wout_back")

        def out_part(c, carry):
            d = jnp.dot(att_t[...], gb_v[:, cols(c)], preferred_element_type=F32)
            b_out[:, :, cols(c)] = d.reshape(n_blocks, -1, BLK).astype(BF16)
            gatt_v[:, cols(c)] = lax.dot_general(
                gb_v[...], wout[cols(c), :], NT, preferred_element_type=F32
            ).astype(BF16)
            return carry

        lax.fori_loop(0, width // BLK, out_part, 0)
        rounds.begin(chunk["out"])
        cos_t, sin_t = rope_v[:, 0:128], rope_v[:, 128:256]

        def pair(hp):
            hc = cols(hp, 128)
            vc = pl.ds(pl.multiple_of(width + hp * 128, 128), 128)
            acc[...] = jnp.zeros_like(acc)
            at = 0
            for half in range(2):
                nk = (half + 1) * pc.g * BLK
                rr = slice(half * BLK, (half + 1) * BLK)
                qp, dop = q_v[rr, hc], gatt_v[rr, hc]
                both = []
                for h in range(2):
                    qm = (jnp.where(lane_mask(h), qp, 0) * 0.125).astype(BF16)
                    dom = jnp.where(lane_mask(h), dop, 0).astype(BF16)
                    s = lax.dot_general(kv_v[0:nk, hc], qm, NT, preferred_element_type=F32)
                    p = jnp.exp(s + bias_v[at : at + nk].astype(F32) - lse_v[hp, h : h + 1, rr])
                    dp = lax.dot_general(kv_v[0:nk, vc], dom, NT, preferred_element_type=F32)
                    weighted = jnp.sum(p * dp, axis=0, keepdims=True)
                    ds = (p * (dp - weighted)).astype(BF16)
                    acc[0:nk, 0:128] += jnp.dot(ds, qm, preferred_element_type=F32)
                    acc[0:nk, 128:256] += jnp.dot(
                        p.astype(BF16), dom, preferred_element_type=F32
                    )
                    both.append(
                        lax.dot_general(kv_v[0:nk, hc], ds, TN, preferred_element_type=F32)
                    )
                sub = lax.broadcasted_iota(jnp.int32, (128, BLK), 0)
                dq = (jnp.where(sub < 64, both[0], both[1]) * 0.125).T
                gqkv[rr, hc] = turned(dq, cos_t[rr], -sin_t[rr]).astype(BF16)
                at += nk
            kv_v[:, hc] = acc[:, 0:128].astype(BF16)
            kv_v[:, vc] = acc[:, 128:256].astype(BF16)

        groups = [rounds.take(n) for n in LOOP_ROUNDS]
        for i, (gy, gx) in enumerate(offsets):
            groups[min(1 + i, 5)].append(
                functools.partial(send_group, functools.partial(to_loader, 0), gy, gx)
            )
        loop_with_steps(HEADS // 2, pair, groups)

    def last_part(gqkv, wqkv):
        load("wqkv_back", full[1], wqkv)
        cos_t, sin_t = rope_v[:, 0:128], rope_v[:, 128:256]
        copies = []
        for o in range(1, pc.g):
            to = (pc.j + o) % pc.g
            for half in range(2):
                where = to if half == 0 else 2 * pc.g - 1 - to
                copies.append(
                    remote(
                        block_at(kv_v, where), dkv_in.at[o - 1, half],
                        dkv_ss.at[half, o - 1], dkv_rs.at[half, o - 1], pc.member(to),
                    )
                )
        start_all(copies)

        def weight_grad(name, base, buf):
            def one(c, carry):
                d = jnp.dot(
                    n1_t[...], gqkv[:, pl.ds(pl.multiple_of(base + c * BLK, BLK), BLK)],
                    preferred_element_type=F32,
                )
                buf[:, :, cols(c)] = d.reshape(n_blocks, -1, BLK).astype(BF16)
                return carry

            lax.fori_loop(0, width // BLK, one, 0)
            rounds.begin(chunk[name])

        while any(t in (chunk["gate0"], chunk["up0"], chunk["gate1"]) and st < 3 for t, st in rounds.todo):
            rounds.run()
        weight_grad("q", 0, b_gate0)
        rounds.run(2)
        wait_arrived(copies)
        rounds.push(chunk["q"])
        for half in range(2):
            own = pl.ds(pl.multiple_of(layer_rows(pc, half) * BLK, BLK), BLK)
            rr = slice(half * BLK, (half + 1) * BLK)
            for i in range(2 * width // BLK):
                cc = slice(i * BLK, (i + 1) * BLK)
                total = kv_v[own, cc].astype(F32)
                for o in range(1, pc.g):
                    total = total + dkv_in[o - 1, half, :, cc].astype(F32)
                if i < width // BLK:
                    total = turned(total, cos_t[rr], -sin_t[rr])
                gqkv[rr, width + i * BLK : width + (i + 1) * BLK] = total.astype(BF16)
        weight_grad("k", width, b_up0)
        weight_grad("v", 2 * width, b_gate1)
        rounds.push(chunk["k"])
        rounds.run(2)
        ready("wqkv_back")
        gn1 = lax.dot_general(gqkv[...], wqkv[...], NT, preferred_element_type=F32)
        x = x_v[...].astype(F32)
        back, d_gain = norm_back(gn1, x, inverse_rms(x), gain_v[0:1])
        dg_v[0:1] = d_gain.reshape(1, width)
        gb_v[...] = (hid_v[...] + back).astype(BF16)
        send_back(1)
        rounds.push(chunk["v"])
        row = lax.broadcasted_iota(jnp.int32, (b_gain.shape[0] * b_gain.shape[1], width), 0)
        col = lax.broadcasted_iota(jnp.int32, row.shape, 1)
        spread = jnp.where(row % SLOTS == 0, dg_v[0:1], jnp.where(row % SLOTS == 1, dg_v[1:2], 0.0))
        spread = jnp.where(row // SLOTS == col // share, spread, 0.0).astype(BF16)
        lane = lax.broadcasted_iota(jnp.int32, (width, 128), 1)
        col = lax.broadcasted_iota(jnp.int32, (width, 128), 0)
        tiles = jnp.dot(spread, (col % share == lane).astype(BF16), preferred_element_type=F32)
        b_gain[...] = tiles.reshape(b_gain.shape).astype(BF16)
        rounds.begin(chunk["gain"])
        rounds.run(4)
        rounds.push(chunk["gain"])
        place_tokens(0)
        for cp in copies:
            cp.wait_send()

    def attention_backward(gqkv):
        pl.run_scoped(
            functools.partial(head_pairs, gqkv),
            pltpu.VMEM((width, width), BF16), pltpu.VMEM((rows, width), BF16),
            pltpu.VMEM((pc.g * rows, 256), F32),
        )
        pl.run_scoped(
            functools.partial(last_part, gqkv), pltpu.VMEM((width, 3 * width), BF16)
        )

    pl.run_scoped(attention_backward, pltpu.VMEM((rows, 3 * width), BF16))
    rounds.finish()
    place_tokens(1)
    len_copy().wait_send()
    gather.wait_sent()
    scatter.wait_sent()
    for t in range(2):
        fin_copy(t).wait()


def layer(ndp, nctx, pre, share, order, lens, freq, x, dy, shards):
    nz, na, nb, g = nctx // pre, ndp // 4, 2, nctx // 2
    n_blocks = ndp * nz
    rows, width = 2 * BLK, x.shape[-1]
    ff = shards[3].shape[1]
    r, rd, rg = width // n_blocks, ff // n_blocks, SLOTS * pre
    dma = pltpu.SemaphoreType.DMA
    chunks = [(0, 0, 128)]
    chunks += [(1, width, width), (1, 2 * width, width), (1, 0, width), (2, 0, width)]
    chunks += [(5, 0, width // 2), (5, width // 2, width // 2)]
    chunks += [(a, c * (ff // 2), ff // 2) for c in range(2) for a in (3, 4)]
    m = len(chunks)
    full = [jax.ShapeDtypeStruct((n_blocks * s.shape[0], s.shape[1]), BF16) for s in shards]
    out_shape = full + [jax.ShapeDtypeStruct((2, BLK, width), BF16)] * 2
    out_shape += [
        jax.ShapeDtypeStruct(s, F32)
        for s in ((r, 3 * width), (r, width), (r, ff), (r, ff), (rd, width), (rg, 128))
    ]
    specs = dict(
        gate0=(r, ff // 2), up0=(r, ff // 2), gate1=(r, ff // 2), up1=(r, ff // 2),
        down0=(rd, width // 3), down1=(rd, width // 3), down2=(rd, width // 3), out=(r, width),
        q=(r, width), k=(r, width), v=(r, width), gain=(rg, 128),
    )
    spec = [specs[name] for name in CHUNKS]
    n = len(CHUNKS)
    scratch = [pltpu.VMEM((n_blocks, r, ff // 2), BF16)] * 4
    scratch += [
        pltpu.VMEM((n_blocks, rd, width), BF16), pltpu.VMEM((n_blocks, r, width), BF16),
        pltpu.VMEM((n_blocks, rg, 128), BF16),
    ]
    scratch += [pltpu.VMEM((na, nb, nz) + s, BF16) for s in spec]
    scratch += [pltpu.VMEM((na - 1, nb - 1, nz // 2) + s, BF16) for s in spec]
    scratch += [pltpu.VMEM((na - 1, nb - 1, nz // 2) + s, BF16) for s in spec]
    scratch += [pltpu.VMEM((nb - 1, nz) + s, BF16) for s in spec]
    scratch += [pltpu.VMEM((na - 1, nz) + s, BF16) for s in spec]
    scratch += [pltpu.VMEM((nz - 1,) + s, BF16) for s in spec]
    scratch += [
        pltpu.VMEM((rows, width), BF16), pltpu.VMEM((rows, width), BF16),
        pltpu.VMEM((g * rows, 2 * width), BF16), pltpu.VMEM((g - 1, 2, BLK, 2 * width), BF16),
        pltpu.VMEM((2, 2, BLK, width), BF16), pltpu.VMEM(lens.shape, lens.dtype),
        pltpu.VMEM((rows, width), F32), pltpu.VMEM((rows, width), BF16),
        pltpu.VMEM((HEADS // 2, 2, rows), F32), pltpu.VMEM((width, rows), BF16),
        pltpu.VMEM((width, rows), BF16), pltpu.VMEM((rows, 256), F32),
        pltpu.VMEM((3 * g * BLK, BLK), BF16), pltpu.VMEM((rows, width), BF16),
        pltpu.VMEM((rows, width), BF16), pltpu.VMEM((8, width), F32), pltpu.VMEM((8, width), F32),
        pltpu.VMEM(full[0].shape, BF16),
        dma((2, 2, ndp)), dma((2, 2, ndp)), dma((2, 2, ndp)), dma((2, 2, ndp)), dma, dma,
        dma((2, 2, g - 1)), dma((2, 2, g - 1)), dma((2, g - 1)), dma((2, g - 1)),
        dma((16,)), dma((2,)),
        dma((m,)), dma((m, nz - 1)), dma((m, nz - 1)),
        dma((m, nb - 1)), dma((m, nb - 1)), dma((m, na - 1)), dma((m, na - 1)),
        dma((m, nb - 1, na - 1)), dma((m, nb - 1, na - 1)),
        dma((m, nb - 1, na - 1)), dma((m, nb - 1, na - 1)),
        dma((m, na, nb)), dma((m, na, nb)),
        dma((n, na, nb)), dma((n, na, nb)),
        dma((n, na - 1, nb - 1)), dma((n, na - 1, nb - 1)),
        dma((n, na - 1, nb - 1)), dma((n, na - 1, nb - 1)),
        dma((n, nb - 1)), dma((n, nb - 1)), dma((n, na - 1)), dma((n, na - 1)),
        dma((n, nz - 1)), dma((n, nz - 1)),
    ]
    res = pl.pallas_call(
        functools.partial(layer_kernel, ndp, nctx, pre, share, chunks),
        out_shape=out_shape,
        in_specs=[VM] * 3 + [ANY] * (2 + len(shards)),
        out_specs=[ANY] * (len(shards) + 2) + [VM] * 6,
        scratch_shapes=scratch,
        compiler_params=pltpu.CompilerParams(
            collective_id=0, has_side_effects=True, vmem_limit_bytes=63 << 20
        ),
        name="layer",
    )(order, lens, freq, x, dy, *shards)
    return res[len(shards) :]


def per_device(
    inputs, cotangent, lengths, send_order,
    norm1_gain, qkv_weight, out_weight, norm2_gain, gate_weight, up_weight, down_weight,
):
    ndp, nctx = lax.axis_size("dp"), lax.axis_size("ctx")
    head = inputs.shape[2] // HEADS
    share = norm1_gain.shape[0]
    pre = 1
    while (share * pre) % 8:
        pre *= 2
    pad = jnp.pad(jnp.stack([norm1_gain, norm2_gain]), ((0, SLOTS - 2), (0, 128 - share)))
    lens = jnp.pad(lengths[:, 0], ((0, 6), (0, 128 - lengths.shape[2])))
    shards = [pad, qkv_weight, out_weight, gate_weight, up_weight, down_weight]
    teams = [[t * pre + i for i in range(pre)] for t in range(nctx // pre)]
    if pre > 1:
        shards = [
            lax.all_gather(w, "ctx", axis_index_groups=teams, axis=0, tiled=True) for w in shards
        ]
    half = head // 2
    frequency = np.float32(rope_base) ** (-(np.arange(half, dtype=np.float32) * 2.0 / head))
    frequency = np.tile(frequency.astype(np.float32), (8, 128 // half))
    fin_out, fin_gin, *owned = layer(
        ndp, nctx, pre, share, send_order, lens, frequency, inputs, cotangent, shards
    )
    if pre > 1:
        owned = [
            lax.psum_scatter(w, "ctx", axis_index_groups=teams, scatter_dimension=0, tiled=True)
            for w in owned
        ]
    s_qkv, s_out, s_gate, s_up, s_down, s_gains = owned
    return (
        fin_out, fin_gin, s_gains[0, :share], s_qkv, s_out, s_gains[1, :share],
        s_gate, s_up, s_down,
    )


def solution(mesh):
    both = ("dp", "ctx")
    in_specs = (
        P(None, both, None), P(None, both, None), P(None, "dp", None), P(None, both, None),
        P(both), P(both, None), P(both, None), P(both), P(both, None), P(both, None), P(both, None),
    )
    out_specs = (
        P(None, both, None), P(None, both, None),
        P(both), P(both, None), P(both, None), P(both), P(both, None), P(both, None), P(both, None),
    )
    return jax.shard_map(
        per_device, mesh=mesh, in_specs=in_specs, out_specs=out_specs, check_vma=False
    )
```

time: 1520 us -> 220 us (0.14)
  waiting for transfers between devices: 881 us -> 0 us
  matrix products: 331 us -> 0 us
  Pallas kernels: 0 us -> 206 us
  local copies, waits for them, and re-layouts: 114 us -> 10 us
  blocking collectives: 92.2 us -> 0 us
  other arithmetic: 40.3 us -> 1.26 us
  starting transfers between devices: 34.4 us -> 0 us
    reduce_scatter x9 -> x0, waiting for transfers between devices: 576 us -> none  [the longest x1 124 us: per_device(): lax.psum_scatter(grad_terms[1], ('dp', 'ctx'), scatter_dimension=0, tiled...]
    dot_general x198 -> x0, matrix products: 331 us -> none  [the longest x24 45 us: head_backward(): jnp.dot(grad_scores, keys, preferred_element_type=jnp.float32) * score_scale]
    all_gather x7 -> x0, waiting for transfers between devices: 291 us -> none  [the longest x2 109 us: per_device(): gathered = lax.all_gather(key_value, 'ctx', axis=0, tiled=True)]
    pallas_call x0 -> x1, Pallas kernels: none -> 206 us  [layer(): pl.pallas_call(functools.partial(layer_kernel, ndp, nctx, pre, share, chu...]
    unnamed x2 -> x0, blocking collectives: 82.2 us -> none
    all_to_all x7 -> x0, starting transfers between devices: 32.9 us -> none  [the longest x2 10.3 us: per_device(): lax.all_to_all(grad_input.reshape(peer_count, slot_rows, model_width), 'd...]
    unnamed x190 -> x17, local copies, waits for them, and re-layouts: 34.4 us -> 7.49 us
    slice x15 -> x0, local copies, waits for them, and re-layouts: 25 us -> none  [the longest x4 11.3 us: per_device(): value_heads = split_heads(gathered[:, model_width:], HEADS)]
  transfers between devices with their start and end apart: 23 -> 0, of which waited for: 19 -> 0; matrix products, arithmetic and copies ran while one was open for 14% -> 0% of each run, Pallas kernels for 0% -> 0%
where the time goes in v2:
time: 220 us; the launch traced here: 218 us
  Pallas kernels  206 us (94%)
  local copies, waits for them, and re-layouts  10 us (5%)
    pallas_call x1, Pallas kernels, layer(): pl.pallas_call(functools.partial(layer_kernel, ndp, nctx, pre, share, chu...  206 us
    unnamed x17, local copies, waits for them, and re-layouts  7.49 us

profile of v2, /device:TPU:4, one launch (start us, length us, event | category | flops | bytes accessed | tf_op | source)
XLA Modules:
  0.0 217.9 jit_solution(10206132431314214485)
XLA Ops:
  0.6 1.3 fusion.5.refs_0_
  1.9 1.3 pad.8.len_ref
  3.2 205.9 %layer.1 = (bf16[256,128]{1,0:T(8,128)(2,1)}, bf16[768,2304]{1,0:T(8,128)(2,1)}, bf16[768,768]{1,0:T(8,128)(2,1)}, bf16[768,2048]{1,0:T(8,128)(2,1)}, bf16[768,2...) custom-call(s32[2,1,256]{2,1,0:T(1,128)} %order_ref.1, ...), custom_call_target="tpu_custom_call" | custom-call | tf_op jit(solution)/shard_map/layer/pallas_call | solution.py:1191
  209.1 0.0 copy-start
  209.1 0.0 copy-start.4
  209.1 0.0 copy-start.3
  209.1 0.0 copy-start.2
  209.1 0.0 copy-start.1
  209.2 1.3 slice_bitcast_fusion
  210.4 2.1 copy.28
  212.5 2.1 copy.29
  214.5 0.0 copy-done
  214.6 0.7 copy.30
  215.2 0.0 copy-done.4
  215.2 0.6 copy.31
  215.9 0.0 copy-done.3
  215.9 0.7 copy.32
  216.6 0.0 copy-done.2
  216.6 0.7 copy.33
  217.2 0.0 copy-done.1
  217.2 0.7 copy.34
Async XLA Ops:
  209.1 5.5 %copy-start = (f32[24,2304]{1,0:T(8,128)S(1)}, f32[24,2304]{1,0:T(8,128)}, u32[]{:S(2)}) copy-start(f32[24,2304]{1,0:T(8,128)} %get-tuple-element.39) | copy-start | bytes 663556
  209.1 6.1 %copy-start.4 = (f32[24,768]{1,0:T(8,128)S(1)}, f32[24,768]{1,0:T(8,128)}, u32[]{:S(2)}) copy-start(f32[24,768]{1,0:T(8,128)} %get-tuple-element.40) | copy-start | bytes 221188
  209.1 6.8 %copy-start.3 = (f32[24,2048]{1,0:T(8,128)S(1)}, f32[24,2048]{1,0:T(8,128)}, u32[]{:S(2)}) copy-start(f32[24,2048]{1,0:T(8,128)} %get-tuple-element.42) | copy-start | bytes 589828
  209.1 7.4 %copy-start.2 = (f32[24,2048]{1,0:T(8,128)S(1)}, f32[24,2048]{1,0:T(8,128)}, u32[]{:S(2)}) copy-start(f32[24,2048]{1,0:T(8,128)} %get-tuple-element.43) | copy-start | bytes 589828
  209.1 8.1 %copy-start.1 = (f32[64,768]{1,0:T(8,128)S(1)}, f32[64,768]{1,0:T(8,128)}, u32[]{:S(2)}) copy-start(f32[64,768]{1,0:T(8,128)} %get-tuple-element.44) | copy-start | bytes 589828

commit v3 on v2

--- a/solution.py
+++ b/solution.py
@@ -566,45 +566,56 @@
     )
 
 
-AHEAD = 5
-BEFORE_X = ('xy', 4)
+FF_STEPS = (((2, 0), (2, 0)), ((2, 1), (2, 1), (2, 0)), ((0, 2), (0, 2), (0, 1)))
+AHEAD = 6
+BEFORE_X = ("xy", 5)
 STRAIGHT = 4
-LOOP_ROUNDS = (2, 2, 2, 1, 1, 1)
+LOOP_ROUNDS = (2, 2, 2, 2, 3, 2)
 ORDER_BEFORE = ()
-ORDER_AT = {0: (0,), 1: (1,), 2: (2,), 3: (3,), 4: (4,), 5: (5,), 6: (6,), 7: (7,)}
-CHUNKS = ("gate0", "up0", "gate1", "up1", "down0", "down1", "down2", "out", "q", "k", "v", "gain")
+ORDER_AT = {0: (0,), 2: (1,), 3: (2,), 4: (3,), 5: (4,), 6: (5,), 7: (6,), 8: (7,)}
+PARTS = ((0, 2), (2, 3), (5, 3))
+CHUNKS = ("gate0", "up0", "gate1", "up1", "gate2", "up2")
+CHUNKS += ("down0", "down1", "down2", "out", "q", "k", "v", "gain")
 
 
 def layer_kernel(
-    ndp, nctx, pre, share, chunks, order_ref, len_ref, freq_ref, x_hbm, dy_hbm, *refs
+    ndp, nctx, pre, share, chunks, order_ref, raw_len_ref, freq_ref, gain1_ref, gain2_ref, x_hbm, dy_hbm, *refs
 ):
     nt, nch = 6, len(CHUNKS)
-    shards, refs = refs[:nt], refs[nt:]
+    made_here = pre == 1
+    shards, refs = refs[: nt - made_here], refs[nt - made_here :]
     full, refs = refs[:nt], refs[nt:]
     fin, refs = refs[:2], refs[2:]
     (s_qkv, s_out, s_gate, s_up, s_down, s_gain), refs = refs[:6], refs[6:]
-    (b_gate0, b_up0, b_gate1, b_up1, b_down, b_out, b_gain), refs = refs[:7], refs[7:]
+    (b_gate0, b_up0, b_gate1, b_up1, b_gate2, b_up2, b_down, b_out, b_gain), refs = refs[:9], refs[9:]
     bufs = [refs[i * nch : (i + 1) * nch] for i in range(6)]
     refs = refs[6 * nch :]
     (
         x_v, dy_v, kv_v, dkv_in, tok, plen, hid_v, q_v, lse_v, att_t, n1_t, rope_v, bias_v, gb_v, out_v,
-        gain_v, dg_v, tiles_v,
+        gain_v, dg_v, tiles_v, len_ref, pad_v,
         tok_ss, tok_rs, ret_ss, ret_rs, len_ss, len_rs, kv_ss, kv_rs, dkv_ss, dkv_rs, load_sem, fin_sem,
         *sems,
     ) = refs
     pc = Place(ndp, nctx, pre)
     rows, width = x_v.shape
     ff = s_gate.shape[1]
-    half_ff, third = ff // 2, width // 3
+    third = width // 3
     slot = BLK // ndp
     n_blocks = ndp * pc.nz
+    len_ref[...] = jnp.zeros_like(len_ref)
+    len_ref[0 : raw_len_ref.shape[0], 0 : raw_len_ref.shape[1]] = raw_len_ref[...]
+    if made_here:
+        gain_v[...] = jnp.zeros_like(gain_v)
+        gain_v[0:1, 0:share] = gain1_ref[...].astype(F32)
+        gain_v[1:2, 0:share] = gain2_ref[...].astype(F32)
+        pad_v[...] = gain_v[:, 0:128].astype(BF16)
+        shards = (pad_v,) + tuple(shards)
     gather = Gather(pc, shards, full, chunks, sems[:13])
     narrow = slice(0, width)
-    grads = [b_gate0, b_up0, b_gate1, b_up1]
+    grads = [b_gate0, b_up0, b_gate1, b_up1, b_gate2, b_up2]
     grads += [b_down.at[:, :, i * third : (i + 1) * third] for i in range(3)] + [b_out]
-    grads += [b.at[:, :, narrow] for b in (b_gate0, b_up0, b_gate1)] + [b_gain]
-    shares = [s_gate.at[:, pl.ds(0, half_ff)], s_up.at[:, pl.ds(0, half_ff)]]
-    shares += [s_gate.at[:, pl.ds(half_ff, half_ff)], s_up.at[:, pl.ds(half_ff, half_ff)]]
+    grads += [b.at[:, :, narrow] for b in (b_gate1, b_up1, b_gate2)] + [b_gain]
+    shares = [ref.at[:, pl.ds(u * BLK, n * BLK)] for u, n in PARTS for ref in (s_gate, s_up)]
     shares += [s_down.at[:, pl.ds(i * third, third)] for i in range(3)] + [s_out]
     shares += [s_qkv.at[:, pl.ds(i * width, width)] for i in range(3)] + [s_gain]
     scatter = Scatter(pc, grads, shares, bufs, sems[13:])
@@ -690,8 +701,6 @@
             tokens_sent(functools.partial(to_loader, t, half))
         for m in range(2):
             tokens_arrived(tok.at[t, m], lambda d, m=m: ret_rs.at[t, m, d], 0)
-            hot = (lax.broadcasted_iota(jnp.int32, (BLK, BLK), 0) == order_ref[m]).astype(BF16)
-            tok[t, m] = jnp.dot(hot, tok[t, m], preferred_element_type=F32).astype(BF16)
         fin_copy(t).start()
 
     steps = Steps()
@@ -921,12 +930,11 @@
         steps.run(2)
         steps.until(("c", last_of[5]))
         load("wdown", full[5], wdown)
-        n_half = half_ff // BLK
         per = BLK // b_down.shape[1]
 
         def part(which, c):
             cc = cols(c)
-            rr = cols(which * n_half + c)
+            rr = cols(PARTS[which][0] + c)
             g = jnp.dot(n2_v[...], wgate[:, cc], preferred_element_type=F32)
             u = jnp.dot(n2_v[...], wup[:, cc], preferred_element_type=F32)
             gi = lax.dot_general(dy_v[...], wdown[rr, :], NT, preferred_element_type=F32)
@@ -939,30 +947,35 @@
             gn2[...] += lax.dot_general(
                 gg, wgate[:, cc], NT, preferred_element_type=F32
             ) + lax.dot_general(gu, wup[:, cc], NT, preferred_element_type=F32)
-            for buf, value in (((b_gate0, b_gate1)[which], gg), ((b_up0, b_up1)[which], gu)):
+            for buf, value in (((b_gate0, b_gate1, b_gate2)[which], gg), ((b_up0, b_up1, b_up2)[which], gu)):
                 d = jnp.dot(n2_t[...], value, preferred_element_type=F32)
                 buf[:, :, cc] = d.reshape(n_blocks, -1, BLK).astype(BF16)
             d = jnp.dot(inner.T, dy_v[...], preferred_element_type=F32)
-            b_down[pl.ds((which * n_half + c) * per, per)] = d.reshape(per, -1, width).astype(BF16)
-
-        def load_half(which):
+            b_down[pl.ds((PARTS[which][0] + c) * per, per)] = d.reshape(per, -1, width).astype(BF16)
+
+        def load_part(which):
             n = len(chunks)
-            steps.until(("c", n - 3 if which == 0 else n - 1))
-            cc = pl.ds(which * half_ff, half_ff)
-            load(f"wgate{which}", full[3].at[:, cc], wgate)
-            load(f"wup{which}", full[4].at[:, cc], wup)
+            steps.until(("c", n - 5 + 2 * which))
+            at, count = PARTS[which]
+            src, dst = pl.ds(at * BLK, count * BLK), pl.ds(0, count * BLK)
+            load(f"wgate{which}", full[3].at[:, src], wgate.at[:, dst])
+            load(f"wup{which}", full[4].at[:, src], wup.at[:, dst])
             ready(f"wgate{which}", f"wup{which}")
 
-        load_half(0)
-        ready("wdown")
-        loop_with_steps(n_half, functools.partial(part, 0), [steps.take(2) for _ in range(n_half)])
-        rounds.begin(chunk["gate0"])
-        rounds.begin(chunk["up0"])
-        load_half(1)
+        for which, (_at, count) in enumerate(PARTS):
+            load_part(which)
+            if which == 0:
+                ready("wdown")
+            groups = []
+            for i in range(count):
+                gathers, sums = FF_STEPS[which][i]
+                groups.append(steps.take(gathers) + rounds.take(sums))
+            loop_with_steps(count, functools.partial(part, which), groups)
+            rounds.begin(chunk[f"gate{which}"])
+            rounds.begin(chunk[f"up{which}"])
         while steps.todo:
             steps.run()
-        loop_with_steps(n_half, functools.partial(part, 1), [rounds.take(2) if i < 2 else [] for i in range(n_half)])
-        for name in ("gate1", "up1", "down0", "down1", "down2"):
+        for name in ("down0", "down1", "down2"):
             rounds.begin(chunk[name])
         out_v[...] = res[...].astype(BF16)
         hid = hid_v[...]
@@ -971,12 +984,12 @@
         gh = dy_v[...].astype(F32) + back
         hid_v[...] = gh
         gb_v[...] = gh.astype(BF16)
-        rounds.push(*[chunk[name] for name in ("gate1", "up1", "down0", "down1", "down2")])
+        rounds.push(*[chunk[name] for name in ("gate2", "up2", "down0", "down1", "down2")])
 
     pl.run_scoped(
         feed_forward,
-        pltpu.VMEM((ff, width), BF16), pltpu.VMEM((width, half_ff), BF16),
-        pltpu.VMEM((width, half_ff), BF16), pltpu.VMEM((rows, width), BF16),
+        pltpu.VMEM((ff, width), BF16), pltpu.VMEM((width, 3 * BLK), BF16),
+        pltpu.VMEM((width, 3 * BLK), BF16), pltpu.VMEM((rows, width), BF16),
         pltpu.VMEM((width, rows), BF16), pltpu.VMEM((rows, width), F32), pltpu.VMEM((rows, width), F32),
     )
 
@@ -1064,9 +1077,9 @@
             lax.fori_loop(0, width // BLK, one, 0)
             rounds.begin(chunk[name])
 
-        while any(t in (chunk["gate0"], chunk["up0"], chunk["gate1"]) and st < 3 for t, st in rounds.todo):
+        while any(t in (chunk["gate1"], chunk["up1"], chunk["gate2"]) and st < 3 for t, st in rounds.todo):
             rounds.run()
-        weight_grad("q", 0, b_gate0)
+        weight_grad("q", 0, b_gate1)
         rounds.run(2)
         wait_arrived(copies)
         rounds.push(chunk["q"])
@@ -1081,8 +1094,8 @@
                 if i < width // BLK:
                     total = turned(total, cos_t[rr], -sin_t[rr])
                 gqkv[rr, width + i * BLK : width + (i + 1) * BLK] = total.astype(BF16)
-        weight_grad("k", width, b_up0)
-        weight_grad("v", 2 * width, b_gate1)
+        weight_grad("k", width, b_up1)
+        weight_grad("v", 2 * width, b_gate2)
         rounds.push(chunk["k"])
         rounds.run(2)
         ready("wqkv_back")
@@ -1128,7 +1141,56 @@
         fin_copy(t).wait()
 
 
-def layer(ndp, nctx, pre, share, order, lens, freq, x, dy, shards):
+def finish_kernel(n, share, order_ref, *refs):
+    tokens, kept, refs = refs[:2], refs[2 : 2 + n], refs[2 + n :]
+    outs, copies, refs = refs[:2], refs[2 : 2 + n + (n > 0)], refs[2 + n + (n > 0) :]
+    tok, fin, in_sem, out_sem, *held = refs
+    moves = [pltpu.make_async_copy(tokens[t], tok.at[t], in_sem.at[t]) for t in range(2)]
+    moves += [pltpu.make_async_copy(kept[i], held[i], in_sem.at[2 + i]) for i in range(n)]
+    start_all(moves)
+    away = []
+    for t in range(2):
+        moves[t].wait()
+        for m in range(2):
+            hot = (lax.broadcasted_iota(jnp.int32, (BLK, BLK), 0) == order_ref[m]).astype(BF16)
+            fin[t, m] = jnp.dot(hot, tok[t, m], preferred_element_type=F32).astype(BF16)
+        away.append(pltpu.make_async_copy(fin.at[t], outs[t], out_sem.at[t]))
+        away[-1].start()
+    for i in range(n - 1):
+        moves[2 + i].wait()
+        away.append(pltpu.make_async_copy(held[i], copies[i], out_sem.at[2 + i]))
+        away[-1].start()
+    if n:
+        moves[1 + n].wait()
+        for i, dst in enumerate(copies[n - 1 :]):
+            dst[...] = held[n - 1][i : i + 1, 0:share]
+    for cp in away:
+        cp.wait()
+
+
+def finish(share, order, tokens, kept):
+    n = len(kept)
+    out = [jax.ShapeDtypeStruct(v.shape, v.dtype) for v in list(tokens) + list(kept[:-1])]
+    specs = [ANY] * len(out)
+    if n:
+        out += [jax.ShapeDtypeStruct((1, share), F32)] * 2
+        specs += [VM] * 2
+    return pl.pallas_call(
+        functools.partial(finish_kernel, n, share),
+        out_shape=out,
+        in_specs=[VM] + [ANY] * (2 + n),
+        out_specs=specs,
+        scratch_shapes=[
+            pltpu.VMEM((2,) + tokens[0].shape, BF16), pltpu.VMEM((2,) + tokens[0].shape, BF16),
+            pltpu.SemaphoreType.DMA((2 + n,)), pltpu.SemaphoreType.DMA((2 + n,)),
+        ]
+        + [pltpu.VMEM(v.shape, v.dtype) for v in kept],
+        compiler_params=pltpu.CompilerParams(vmem_limit_bytes=63 << 20),
+        name="finish",
+    )(order, *tokens, *kept)
+
+
+def layer(ndp, nctx, pre, share, order, lens, freq, gains, x, dy, shards):
     nz, na, nb, g = nctx // pre, ndp // 4, 2, nctx // 2
     n_blocks = ndp * nz
     rows, width = 2 * BLK, x.shape[-1]
@@ -1138,8 +1200,9 @@
     chunks = [(0, 0, 128)]
     chunks += [(1, width, width), (1, 2 * width, width), (1, 0, width), (2, 0, width)]
     chunks += [(5, 0, width // 2), (5, width // 2, width // 2)]
-    chunks += [(a, c * (ff // 2), ff // 2) for c in range(2) for a in (3, 4)]
+    chunks += [(a, u * BLK, n * BLK) for u, n in PARTS for a in (3, 4)]
     m = len(chunks)
+    given = shards[1:] if pre == 1 else shards
     full = [jax.ShapeDtypeStruct((n_blocks * s.shape[0], s.shape[1]), BF16) for s in shards]
     out_shape = full + [jax.ShapeDtypeStruct((2, BLK, width), BF16)] * 2
     out_shape += [
@@ -1147,13 +1210,13 @@
         for s in ((r, 3 * width), (r, width), (r, ff), (r, ff), (rd, width), (rg, 128))
     ]
     specs = dict(
-        gate0=(r, ff // 2), up0=(r, ff // 2), gate1=(r, ff // 2), up1=(r, ff // 2),
+        **{f"{name}{i}": (r, n * BLK) for i, (_u, n) in enumerate(PARTS) for name in ("gate", "up")},
         down0=(rd, width // 3), down1=(rd, width // 3), down2=(rd, width // 3), out=(r, width),
         q=(r, width), k=(r, width), v=(r, width), gain=(rg, 128),
     )
     spec = [specs[name] for name in CHUNKS]
     n = len(CHUNKS)
-    scratch = [pltpu.VMEM((n_blocks, r, ff // 2), BF16)] * 4
+    scratch = [pltpu.VMEM((n_blocks,) + s, BF16) for s in spec[:6]]
     scratch += [
         pltpu.VMEM((n_blocks, rd, width), BF16), pltpu.VMEM((n_blocks, r, width), BF16),
         pltpu.VMEM((n_blocks, rg, 128), BF16),
@@ -1167,16 +1230,16 @@
     scratch += [
         pltpu.VMEM((rows, width), BF16), pltpu.VMEM((rows, width), BF16),
         pltpu.VMEM((g * rows, 2 * width), BF16), pltpu.VMEM((g - 1, 2, BLK, 2 * width), BF16),
-        pltpu.VMEM((2, 2, BLK, width), BF16), pltpu.VMEM(lens.shape, lens.dtype),
+        pltpu.VMEM((2, 2, BLK, width), BF16), pltpu.VMEM((8, 128), jnp.int32),
         pltpu.VMEM((rows, width), F32), pltpu.VMEM((rows, width), BF16),
         pltpu.VMEM((HEADS // 2, 2, rows), F32), pltpu.VMEM((width, rows), BF16),
         pltpu.VMEM((width, rows), BF16), pltpu.VMEM((rows, 256), F32),
         pltpu.VMEM((3 * g * BLK, BLK), BF16), pltpu.VMEM((rows, width), BF16),
         pltpu.VMEM((rows, width), BF16), pltpu.VMEM((8, width), F32), pltpu.VMEM((8, width), F32),
-        pltpu.VMEM(full[0].shape, BF16),
+        pltpu.VMEM(full[0].shape, BF16), pltpu.VMEM((8, 128), jnp.int32), pltpu.VMEM((SLOTS, 128), BF16),
         dma((2, 2, ndp)), dma((2, 2, ndp)), dma((2, 2, ndp)), dma((2, 2, ndp)), dma, dma,
         dma((2, 2, g - 1)), dma((2, 2, g - 1)), dma((2, g - 1)), dma((2, g - 1)),
-        dma((16,)), dma((2,)),
+        dma((20,)), dma((2,)),
         dma((m,)), dma((m, nz - 1)), dma((m, nz - 1)),
         dma((m, nb - 1)), dma((m, nb - 1)), dma((m, na - 1)), dma((m, na - 1)),
         dma((m, nb - 1, na - 1)), dma((m, nb - 1, na - 1)),
@@ -1191,14 +1254,14 @@
     res = pl.pallas_call(
         functools.partial(layer_kernel, ndp, nctx, pre, share, chunks),
         out_shape=out_shape,
-        in_specs=[VM] * 3 + [ANY] * (2 + len(shards)),
+        in_specs=[VM] * 5 + [ANY] * (2 + len(given)),
         out_specs=[ANY] * (len(shards) + 2) + [VM] * 6,
         scratch_shapes=scratch,
         compiler_params=pltpu.CompilerParams(
             collective_id=0, has_side_effects=True, vmem_limit_bytes=63 << 20
         ),
         name="layer",
-    )(order, lens, freq, x, dy, *shards)
+    )(order, lens, freq, *gains, x, dy, *given)
     return res[len(shards) :]
 
 
@@ -1212,8 +1275,10 @@
     pre = 1
     while (share * pre) % 8:
         pre *= 2
-    pad = jnp.pad(jnp.stack([norm1_gain, norm2_gain]), ((0, SLOTS - 2), (0, 128 - share)))
-    lens = jnp.pad(lengths[:, 0], ((0, 6), (0, 128 - lengths.shape[2])))
+    gains = (norm1_gain.reshape(1, share), norm2_gain.reshape(1, share))
+    pad = jax.ShapeDtypeStruct((SLOTS, 128), BF16)
+    if pre > 1:
+        pad = jnp.pad(jnp.concatenate(gains), ((0, SLOTS - 2), (0, 128 - share)))
     shards = [pad, qkv_weight, out_weight, gate_weight, up_weight, down_weight]
     teams = [[t * pre + i for i in range(pre)] for t in range(nctx // pre)]
     if pre > 1:
@@ -1223,18 +1288,23 @@
     half = head // 2
     frequency = np.float32(rope_base) ** (-(np.arange(half, dtype=np.float32) * 2.0 / head))
     frequency = np.tile(frequency.astype(np.float32), (8, 128 // half))
-    fin_out, fin_gin, *owned = layer(
-        ndp, nctx, pre, share, send_order, lens, frequency, inputs, cotangent, shards
+    back_out, back_gin, *owned = layer(
+        ndp, nctx, pre, share, send_order, lengths[:, 0], frequency, gains, inputs, cotangent, shards
     )
     if pre > 1:
         owned = [
             lax.psum_scatter(w, "ctx", axis_index_groups=teams, scatter_dimension=0, tiled=True)
             for w in owned
         ]
-    s_qkv, s_out, s_gate, s_up, s_down, s_gains = owned
+        fin_out, fin_gin = finish(share, send_order, (back_out, back_gin), [])
+        s_qkv, s_out, s_gate, s_up, s_down, s_gains = owned
+        g1, g2 = s_gains[0:1, :share], s_gains[1:2, :share]
+    else:
+        fin_out, fin_gin, s_qkv, s_out, s_gate, s_up, s_down, g1, g2 = finish(
+            share, send_order, (back_out, back_gin), owned
+        )
     return (
-        fin_out, fin_gin, s_gains[0, :share], s_qkv, s_out, s_gains[1, :share],
-        s_gate, s_up, s_down,
+        fin_out, fin_gin, g1.reshape(share), s_qkv, s_out, g2.reshape(share), s_gate, s_up, s_down,
     )
 
 

time: 220 us -> 213 us (0.968)
  local copies, waits for them, and re-layouts: 10 us -> 0 us
  Pallas kernels: 206 us -> 209 us
    unnamed x17 -> x0, local copies, waits for them, and re-layouts: 7.49 us -> none
    pallas_call x0 -> x1, Pallas kernels: none -> 4.39 us  [finish(): pl.pallas_call(functools.partial(finish_kernel, n, share), out_shape=out,...]
where the time goes in v3:
time: 213 us; the launch traced here: 210 us
  Pallas kernels  209 us (98%)
    pallas_call x1, Pallas kernels, layer(): pl.pallas_call(functools.partial(layer_kernel, ndp, nctx, pre, share, chu...  204 us
    pallas_call x1, Pallas kernels, finish(): pl.pallas_call(functools.partial(finish_kernel, n, share), out_shape=out,...  4.39 us

profile of v3, /device:TPU:4, one launch (start us, length us, event | category | flops | bytes accessed | tf_op | source)
XLA Modules:
  0.0 209.6 jit_solution(4457333299876451713)
XLA Ops:
  0.6 204.4 %layer.1 = (bf16[256,128]{1,0:T(8,128)(2,1)}, bf16[768,2304]{1,0:T(8,128)(2,1)}, bf16[768,768]{1,0:T(8,128)(2,1)}, bf16[768,2048]{1,0:T(8,128)(2,1)}, bf16[768,2...) custom-call(s32[2,1,256]{2,1,0:T(1,128)} %order_ref.3, ...), custom_call_target="tpu_custom_call" | custom-call | tf_op jit(solution)/shard_map/layer/pallas_call | solution.py:1254
  205.0 4.4 %finish.1 = (bf16[2,256,768]{2,1,0:T(8,128)(2,1)}, bf16[2,256,768]{2,1,0:T(8,128)(2,1)}, f32[24,2304]{1,0:T(8,128)}, f32[24,768]{1,0:T(8,128)}, f32[24,2048]{1,0...) custom-call(s32[2,1,256]{2,1,0:T(1,128)} %order_ref.3, ...), custom_call_target="tpu_custom_call" | custom-call | tf_op jit(solution)/shard_map/finish/pallas_call | solution.py:1178
